TPU v7x, 1024 devices: a whole 4x4x32 slice. The times are simulated.
1024 devices in a mesh: dom: 32 (over y, x, core), head: 32 (over z).
Axes of the slice: x: 4, y: 4, z: 32, core: 2. Of those that a mesh axis runs over, the one named last changes fastest.
Arguments:
- queries: bfloat16 [18432, 2048], P(('dom', 'head')), may hold values from -8 to 8
- keys_in: bfloat16 [18432, 2048], P(('dom', 'head')), may hold values from -8 to 8
- values_in: bfloat16 [18432, 2048], P(('dom', 'head')), may hold values from -6 to 6
- grad_out: bfloat16 [18432, 2048], P(('dom', 'head')), may hold values from -6 to 6
- pos_bias: float32 [32, 64, 576], P('head'), may hold values from -4 to 4
- neighbours: int32 [288, 9], P('dom'), may hold values from 0 to 32, as said below
- send_block: int32 [32, 8, 3], P('dom'), may hold values from 0 to 8, as said below
- orient: int32 [32, 8], P('dom'), may hold values from 0 to 7
Outputs:
- grad_q: bfloat16 [18432, 2048], P(('dom', 'head'))
- grad_k: bfloat16 [18432, 2048], P(('dom', 'head'))
- grad_v: bfloat16 [18432, 2048], P(('dom', 'head'))
Inputs may be any that keep to these rules, and one draw needn't show every extreme that they name: `neighbours`: entry [d * 9 + b, j] names the j-th key block of query block b of domain d: e below 9 is the domain's own block e, and 9 + k * 3 + c is slot c of what domain d borrows from direction k. The 9 entries of a query block are distinct and name only live slots of send_block. `send_block`: entry [p, k, c] is the block that domain p lends in slot c to the domain d with nb(d, k) = p. The live slots of one entry [p, k] name distinct blocks; there are 3 of them for the four edge directions and one for the four corner directions, none where no such d exists; slots that are not live hold 0 and no neighbours entry names them.
All inputs are finite; a program needn't handle non-finite values.
Results may differ from a plain program's by a relative error of at most 0.025.
Values may be sent and summed in bfloat16 or wider, within the bound.
A program may use at most 32 MiB of HBM per device.

v0:
```python
import jax
import jax.numpy as jnp
import numpy as np
from jax import lax
from jax.sharding import PartitionSpec as P

HD = 64
PATCH = 8
BT = 64
GRID_ROWS = 4
DIRS = 8
WIN = 9
WINK = 576
QB_DOM = 9
CAP = 3


OFFSET_LIST = [(-1, -1), (-1, 0), (-1, 1), (0, -1), (0, 1), (1, -1), (1, 0), (1, 1)]


def from_behind(value, axis, steps):
    count = lax.axis_size(axis)
    first, last = (max(0, -steps), min(count, count - steps))
    return lax.ppermute(value, axis, [(source, source + steps) for source in range(first, last)])


def patch_tables(patch_side):
    flat_index = np.arange(patch_side * patch_side)
    row_of = flat_index // patch_side
    col_of = flat_index % patch_side
    table_list = []
    for orient_id in range(8):
        row_new = patch_side - 1 - row_of if orient_id % 2 == 1 else row_of
        col_new = patch_side - 1 - col_of if orient_id // 2 % 2 == 1 else col_of
        mapped = (
            patch_side * col_new + row_new if orient_id >= 4 else patch_side * row_new + col_new
        )
        table_list.append(mapped)
    forward = np.stack(table_list).astype(np.int32)
    inverse = np.argsort(forward, axis=1).astype(np.int32)
    return (forward, inverse)


def per_device(queries, keys_in, values_in, grad_out, pos_bias, neighbours, send_block, orient):
    head_local = pos_bias.shape[0]
    score_scale = HD ** (-0.5)
    grid_cols = lax.axis_size("dom") // GRID_ROWS
    slot_total = QB_DOM + DIRS * CAP
    forward, inverse = patch_tables(PATCH)
    query_heads, key_heads, value_heads, grad_heads = (
        lax.all_to_all(queries, "head", split_axis=1, concat_axis=0, tiled=True),
        lax.all_to_all(keys_in, "head", split_axis=1, concat_axis=0, tiled=True),
        lax.all_to_all(values_in, "head", split_axis=1, concat_axis=0, tiled=True),
        lax.all_to_all(grad_out, "head", split_axis=1, concat_axis=0, tiled=True),
    )
    tokens_dom = query_heads.shape[0]

    def split_heads(matrix):
        return matrix.reshape(QB_DOM, BT, head_local, HD)

    own_pairs = jnp.concatenate([split_heads(key_heads), split_heads(value_heads)], axis=-1)
    own_sends = send_block[0].reshape(-1)
    outgoing = own_pairs[own_sends].reshape(DIRS, CAP, BT, head_local, 2 * HD)
    arrived_groups = [None] * DIRS
    for index, (row_step, col_step) in enumerate(OFFSET_LIST):
        arrived_groups[index] = from_behind(
            outgoing[index], "dom", -(row_step * grid_cols + col_step)
        )
    arrived = jnp.stack(arrived_groups).reshape(DIRS * CAP, BT, head_local, 2 * HD)
    turn_index = jnp.repeat(jnp.asarray(forward)[orient[0]], CAP, axis=0)
    oriented = jnp.take_along_axis(arrived, turn_index[:, :, None, None], axis=1)
    extended = jnp.concatenate([own_pairs, oriented], axis=0)
    near_ids = neighbours.reshape(-1)
    window = extended[near_ids].reshape(QB_DOM, WINK, head_local, 2 * HD)
    win_k = window[..., :HD]
    win_v = window[..., HD:]
    query_blk = split_heads(query_heads)
    grad_blk = split_heads(grad_heads)
    scores = (
        jnp.einsum("bthd,bkhd->bhtk", query_blk, win_k, preferred_element_type=jnp.float32)
        * score_scale
        + pos_bias[None]
    )
    row_top = jnp.max(scores, axis=-1, keepdims=True)
    exp_scores = jnp.exp(scores - row_top)
    probs = exp_scores / jnp.sum(exp_scores, axis=-1, keepdims=True)
    probs_half = probs.astype(jnp.bfloat16)
    dprobs = jnp.einsum("bthd,bkhd->bhtk", grad_blk, win_v, preferred_element_type=jnp.float32)
    row_delta = jnp.sum(probs_half.astype(jnp.float32) * dprobs, axis=-1, keepdims=True)
    dscores = (probs * (dprobs - row_delta)).astype(jnp.bfloat16)
    grad_q_blk = (
        jnp.einsum("bhtk,bkhd->bthd", dscores, win_k, preferred_element_type=jnp.float32)
        * score_scale
    )
    grad_q_loc = grad_q_blk.astype(jnp.bfloat16).reshape(tokens_dom, head_local * HD)
    grad_kw = (
        jnp.einsum("bhtk,bthd->bkhd", dscores, query_blk, preferred_element_type=jnp.float32)
        * score_scale
    )
    grad_vw = jnp.einsum(
        "bhtk,bthd->bkhd", probs_half, grad_blk, preferred_element_type=jnp.float32
    )
    window_grad = jnp.concatenate([grad_kw, grad_vw], axis=-1).reshape(
        QB_DOM * WIN, BT, head_local, 2 * HD
    )
    slot_grad = jax.ops.segment_sum(window_grad, near_ids, num_segments=slot_total)
    back_order = jnp.repeat(jnp.asarray(inverse)[orient[0]], CAP, axis=0)
    leaving = jnp.take_along_axis(slot_grad[QB_DOM:], back_order[:, :, None, None], axis=1)
    leaving = leaving.astype(jnp.bfloat16).reshape(DIRS, CAP, BT, head_local, 2 * HD)
    back_groups = [None] * DIRS
    for index, (row_step, col_step) in enumerate(OFFSET_LIST):
        back_groups[index] = from_behind(leaving[index], "dom", row_step * grid_cols + col_step)
    returned = (
        jnp.stack(back_groups).reshape(DIRS * CAP, BT, head_local, 2 * HD).astype(jnp.float32)
    )
    own_grad = slot_grad[:QB_DOM] + jax.ops.segment_sum(returned, own_sends, num_segments=QB_DOM)
    grad_k_loc = own_grad[..., :HD].astype(jnp.bfloat16).reshape(tokens_dom, head_local * HD)
    grad_v_loc = own_grad[..., HD:].astype(jnp.bfloat16).reshape(tokens_dom, head_local * HD)
    return (
        lax.all_to_all(grad_q_loc, "head", split_axis=0, concat_axis=1, tiled=True),
        lax.all_to_all(grad_k_loc, "head", split_axis=0, concat_axis=1, tiled=True),
        lax.all_to_all(grad_v_loc, "head", split_axis=0, concat_axis=1, tiled=True),
    )


def solution(mesh):
    return jax.shard_map(
        per_device,
        mesh=mesh,
        in_specs=(
            P(("dom", "head"), None),
            P(("dom", "head"), None),
            P(("dom", "head"), None),
            P(("dom", "head"), None),
            P("head", None, None),
            P("dom", None),
            P("dom", None, None),
            P("dom", None),
        ),
        out_specs=(P(("dom", "head"), None), P(("dom", "head"), None), P(("dom", "head"), None)),
        check_vma=False,
    )
```

profile of v0, /device:TPU:1, one launch (start us, length us, event | category | flops | bytes accessed | tf_op | source)
XLA Modules:
  0.0 328.6 jit_solution(13307315519439413036)
XLA Ops:
  0.6 1.1 all_to_all.96
  2.6 29.3 %all-to-all-start.2 = ((bf16[32,2,576]{2,1,0:T(2,128)(2,1)}), bf16[32,2,576]{2,1,0:T(2,128)(2,1)S(1)}, u32[]{:S(2)}, u32[]{:S(2)}) async-start(bf16[32,2,576]{2,1,0:T(2,128)(2,1)} %reshape.514), calls=%async_computation.2 | async-start | bytes 163840 | tf_op jit(solution)/shard_map/all_to_all | solution.py:51
  32.6 1.2 gather_fusion
  36.3 1.2 gather_fusion.3
  37.6 1.1 all_to_all.93
  41.8 15.5 %all-to-all-done.2 = bf16[32,2,576]{2,1,0:T(2,128)(2,1)S(1)} async-done(((bf16[32,2,576]{2,1,0:T(2,128)(2,1)}), bf16[32,2,576]{2,1,0:T(2,128)(2,1)S(1)}, u32[]{:S(2)}, u32[]{:S(2)}) %all-to-all-start.2) | async-done | bytes 73760 | tf_op jit(solution)/shard_map/all_to_all | solution.py:51
  57.3 5.8 %all-to-all-start.1 = ((bf16[32,2,576]{2,1,0:T(2,128)(2,1)}), bf16[32,2,576]{2,1,0:T(2,128)(2,1)S(1)}, u32[]{:S(2)}, u32[]{:S(2)}) async-start(bf16[32,2,576]{2,1,0:T(2,128)(2,1)} %reshape.510), calls=%async_computation.1 | async-start | bytes 163840 | tf_op jit(solution)/shard_map/all_to_all | solution.py:53
  63.1 24.3 %all-to-all-done.1 = bf16[32,2,576]{2,1,0:T(2,128)(2,1)S(1)} async-done(((bf16[32,2,576]{2,1,0:T(2,128)(2,1)}), bf16[32,2,576]{2,1,0:T(2,128)(2,1)S(1)}, u32[]{:S(2)}, u32[]{:S(2)}) %all-to-all-start.1) | async-done | bytes 73760 | tf_op jit(solution)/shard_map/all_to_all | solution.py:53
  87.4 4.8 %all-to-all-start = ((bf16[32,2,576]{2,1,0:T(2,128)(2,1)}), bf16[32,2,576]{2,1,0:T(2,128)(2,1)S(1)}, u32[]{:S(2)}, u32[]{:S(2)}) async-start(bf16[32,2,576]{2,1,0:T(2,128)(2,1)} %reshape.512), calls=%async_computation | async-start | bytes 163840 | tf_op jit(solution)/shard_map/all_to_all | solution.py:52
  92.8 23.4 %all-to-all-done = bf16[32,2,576]{2,1,0:T(2,128)(2,1)S(1)} async-done(((bf16[32,2,576]{2,1,0:T(2,128)(2,1)}), bf16[32,2,576]{2,1,0:T(2,128)(2,1)S(1)}, u32[]{:S(2)}, u32[]{:S(2)}) %all-to-all-start) | async-done | bytes 73760 | tf_op jit(solution)/shard_map/all_to_all | solution.py:52
  116.2 3.9 %all-to-all-start.3 = ((bf16[32,2,576]{2,1,0:T(2,128)(2,1)}), bf16[32,2,576]{2,1,0:T(2,128)(2,1)S(1)}, u32[]{:S(2)}, u32[]{:S(2)}) async-start(bf16[32,2,576]{2,1,0:T(2,128)(2,1)} %reshape.508), calls=%async_computation.3 | async-start | bytes 163840 | tf_op jit(solution)/shard_map/all_to_all | solution.py:54
  121.1 8.1 %collective-permute-start = (bf16[3,64,1,128]{3,1,0,2:T(8,128)(2,1)S(1)}, bf16[3,64,1,128]{3,1,0,2:T(8,128)(2,1)S(1)}, u32[]{:S(2)}, u32[]{:S(2)}) collective-permute-start(bf16[3,64,1,128]{3,1,0,2:T(8,128)(2,1)S(1)} %get-tuple-element.18), channel_id=1, source_target_pairs={{0,288},{32,320},{64,352},{96,384},{128,416},{160,448},{192,480},{... | collective-permute-start | bytes 147464 | tf_op jit(solution)/shard_map/ppermute | solution.py:24
  129.2 3.2 collective-permute-start.1
  132.4 1.3 collective-permute-start.2
  133.8 5.0 %collective-permute-start.3 = (bf16[3,64,1,128]{3,1,0,2:T(8,128)(2,1)S(1)}, bf16[3,64,1,128]{3,1,0,2:T(8,128)(2,1)S(1)}, u32[]{:S(2)}, u32[]{:S(2)}) collective-permute-start(bf16[3,64,1,128]{3,1,0,2:T(8,128)(2,1)S(1)} %get-tuple-element.15), channel_id=1, source_target_pairs={{0,32},{32,64},{64,96},{96,128},{128,160},{160,192},{192,224},{224... | collective-permute-start | bytes 147464 | tf_op jit(solution)/shard_map/ppermute | solution.py:24
  138.7 1.9 collective-permute-start.4
  140.7 3.4 %all-to-all-done.3 = bf16[32,2,576]{2,1,0:T(2,128)(2,1)S(1)} async-done(((bf16[32,2,576]{2,1,0:T(2,128)(2,1)}), bf16[32,2,576]{2,1,0:T(2,128)(2,1)S(1)}, u32[]{:S(2)}, u32[]{:S(2)}) %all-to-all-start.3) | async-done | bytes 73760 | tf_op jit(solution)/shard_map/all_to_all | solution.py:54
  144.3 1.3 collective-permute-start.5
  145.6 1.3 collective-permute-start.6
  147.0 1.3 collective-permute-start.7
  148.3 6.2 %collective-permute-done.5 = bf16[3,64,1,128]{3,1,0,2:T(8,128)(2,1)S(1)} collective-permute-done((bf16[3,64,1,128]{3,1,0,2:T(8,128)(2,1)S(1)}, bf16[3,64,1,128]{3,1,0,2:T(8,128)(2,1)S(1)}, u32[]{:S(2)}, u32[]{:S(2)}) %collective-permute-start.5) | collective-permute-done | bytes 49184 | tf_op jit(solution)/shard_map/ppermute | solution.py:24
  154.5 2.7 collective-permute-done.6
  157.3 2.2 collective-permute-done.7
  159.5 8.5 %gather_fusion.4 = bf16[1536,128]{1,0:T(8,128)(2,1)S(1)} fusion(bf16[24,64,128]{2,1,0:T(8,128)(2,1)S(1)} %bitcast.169, s32[1536]{0:T(1024)S(1)} %reshape.453), kind=kCustom, calls=%fused_computation.4 | custom fusion | bytes 798720 | tf_op jit(solution)/shard_map/jit(take_along_axis)/gather | solution.py:71
  168.4 1.9 gather_fusion.2
  170.2 1.9 bitcast_add_fusion
  172.1 1.7 fusion.22
  173.9 2.4 convolution_bitcast_fusion
  176.3 2.1 fusion.2
  180.0 1.0 copy-done.3
  181.2 2.3 copy.46
  183.6 10.0 %scatter_fusion = f32[33,64,128]{2,1,0:T(8,128)S(1)} fusion(f32[33,64,128]{2,1,0:T(8,128)S(1)} %broadcast.212, s32[81]{0:T(128)S(1)} %reshape.471, f32[81,64,128]{2,1,0:T(8,128)} %bitcast.170), kind=kCustom, calls=%fused_computation.6 | custom fusion | flops 663552 | bytes 7962948 | tf_op jit(solution)/shard_map/scatter-add | solution.py:106
  193.7 8.5 %gather_fusion.5 = bf16[1536,128]{1,0:T(8,128)(2,1)S(1)} fusion(bf16[24,64,128]{2,1,0:T(8,128)(2,1)S(1)} %slice.139, s32[1536]{0:T(1024)S(1)} %reshape.461), kind=kCustom, calls=%fused_computation.5 | custom fusion | bytes 798720 | tf_op jit(solution)/shard_map/jit(take_along_axis)/gather | solution.py:108
  202.5 1.6 collective-permute-start.8
  205.7 13.3 %all-to-all-start.4 = ((bf16[32,2,576]{2,1,0:T(2,128)(2,1)}), bf16[32,2,576]{2,1,0:T(2,128)(2,1)S(1)}, u32[]{:S(2)}, u32[]{:S(2)}) async-start(bf16[32,2,576]{2,1,0:T(2,128)(2,1)} %reshape.516), calls=%async_computation.4 | async-start | bytes 163840 | tf_op jit(solution)/shard_map/all_to_all | solution.py:120
  219.1 1.3 collective-permute-start.9
  220.4 1.3 collective-permute-start.10
  221.7 3.3 collective-permute-start.11
  224.9 3.0 collective-permute-start.12
  227.9 7.2 %collective-permute-start.13 = (bf16[3,64,1,128]{3,1,0,2:T(8,128)(2,1)S(1)}, bf16[3,64,1,128]{3,1,0,2:T(8,128)(2,1)S(1)}, u32[]{:S(2)}, u32[]{:S(2)}) collective-permute-start(bf16[3,64,1,128]{3,1,0,2:T(8,128)(2,1)S(1)} %get-tuple-element.5), channel_id=1, source_target_pairs={{0,224},{32,256},{64,288},{96,320},{128,352},{160,384},{192,416},{... | collective-permute-start | bytes 147464 | tf_op jit(solution)/shard_map/ppermute | solution.py:24
  235.1 6.7 %collective-permute-start.14 = (bf16[3,64,1,128]{3,1,0,2:T(8,128)(2,1)S(1)}, bf16[3,64,1,128]{3,1,0,2:T(8,128)(2,1)S(1)}, u32[]{:S(2)}, u32[]{:S(2)}) collective-permute-start(bf16[3,64,1,128]{3,1,0,2:T(8,128)(2,1)S(1)} %get-tuple-element.4), channel_id=1, source_target_pairs={{0,256},{32,288},{64,320},{96,352},{128,384},{160,416},{192,448},{... | collective-permute-start | bytes 147464 | tf_op jit(solution)/shard_map/ppermute | solution.py:24
  241.9 4.9 %collective-permute-start.15 = (bf16[3,64,1,128]{3,1,0,2:T(8,128)(2,1)S(1)}, bf16[3,64,1,128]{3,1,0,2:T(8,128)(2,1)S(1)}, u32[]{:S(2)}, u32[]{:S(2)}) collective-permute-start(bf16[3,64,1,128]{3,1,0,2:T(8,128)(2,1)S(1)} %get-tuple-element.3), channel_id=1, source_target_pairs={{0,288},{32,320},{64,352},{96,384},{128,416},{160,448},{192,480},{... | collective-permute-start | bytes 147464 | tf_op jit(solution)/shard_map/ppermute | solution.py:24
  246.9 1.0 collective-permute-done.15
  248.1 2.1 scatter_fusion.1
  251.2 21.5 %all-to-all-start.5 = ((bf16[32,2,576]{2,1,0:T(2,128)(2,1)}), bf16[32,2,576]{2,1,0:T(2,128)(2,1)S(1)}, u32[]{:S(2)}, u32[]{:S(2)}) async-start(bf16[32,2,576]{2,1,0:T(2,128)(2,1)} %reshape.518), calls=%async_computation.5 | async-start | bytes 163840 | tf_op jit(solution)/shard_map/all_to_all | solution.py:121
  273.5 25.7 %all-to-all-done.5 = bf16[32,2,576]{2,1,0:T(2,128)(2,1)S(1)} async-done(((bf16[32,2,576]{2,1,0:T(2,128)(2,1)}), bf16[32,2,576]{2,1,0:T(2,128)(2,1)S(1)}, u32[]{:S(2)}, u32[]{:S(2)}) %all-to-all-start.5) | async-done | bytes 73760 | tf_op jit(solution)/shard_map/all_to_all | solution.py:121
  299.2 3.9 %all-to-all-start.6 = ((bf16[32,2,576]{2,1,0:T(2,128)(2,1)}), bf16[32,2,576]{2,1,0:T(2,128)(2,1)S(1)}, u32[]{:S(2)}, u32[]{:S(2)}) async-start(bf16[32,2,576]{2,1,0:T(2,128)(2,1)} %reshape.520), calls=%async_computation.6 | async-start | bytes 163840 | tf_op jit(solution)/shard_map/all_to_all | solution.py:122
  305.1 22.5 %all-to-all-done.6 = bf16[32,2,576]{2,1,0:T(2,128)(2,1)S(1)} async-done(((bf16[32,2,576]{2,1,0:T(2,128)(2,1)}), bf16[32,2,576]{2,1,0:T(2,128)(2,1)S(1)}, u32[]{:S(2)}, u32[]{:S(2)}) %all-to-all-start.6) | async-done | bytes 73760 | tf_op jit(solution)/shard_map/all_to_all | solution.py:122
  (119 shorter events, 18.2 us)
Async XLA Ops:
  0.6 39.0 %copy-start.5 = (bf16[18,2048]{1,0:T(8,128)(2,1)S(1)}, bf16[18,2048]{1,0:T(8,128)(2,1)}, u32[]{:S(2)}) copy-start(bf16[18,2048]{1,0:T(8,128)(2,1)} %param.11) | copy-start | bytes 221188
  1.8 38.9 %copy-start.6 = (bf16[18,2048]{1,0:T(8,128)(2,1)S(1)}, bf16[18,2048]{1,0:T(8,128)(2,1)}, u32[]{:S(2)}) copy-start(bf16[18,2048]{1,0:T(8,128)(2,1)} %param.13) | copy-start | bytes 221188
  2.6 54.7 %all-to-all-start.2 = ((bf16[32,2,576]{2,1,0:T(2,128)(2,1)}), bf16[32,2,576]{2,1,0:T(2,128)(2,1)S(1)}, u32[]{:S(2)}, u32[]{:S(2)}) async-start(bf16[32,2,576]{2,1,0:T(2,128)(2,1)} %reshape.514), calls=%async_computation.2 | async-start | bytes 163840 | tf_op jit(solution)/shard_map/all_to_all | solution.py:51
  57.3 30.1 %all-to-all-start.1 = ((bf16[32,2,576]{2,1,0:T(2,128)(2,1)}), bf16[32,2,576]{2,1,0:T(2,128)(2,1)S(1)}, u32[]{:S(2)}, u32[]{:S(2)}) async-start(bf16[32,2,576]{2,1,0:T(2,128)(2,1)} %reshape.510), calls=%async_computation.1 | async-start | bytes 163840 | tf_op jit(solution)/shard_map/all_to_all | solution.py:53
  87.4 28.7 %all-to-all-start = ((bf16[32,2,576]{2,1,0:T(2,128)(2,1)}), bf16[32,2,576]{2,1,0:T(2,128)(2,1)S(1)}, u32[]{:S(2)}, u32[]{:S(2)}) async-start(bf16[32,2,576]{2,1,0:T(2,128)(2,1)} %reshape.512), calls=%async_computation | async-start | bytes 163840 | tf_op jit(solution)/shard_map/all_to_all | solution.py:52
  116.2 27.9 %all-to-all-start.3 = ((bf16[32,2,576]{2,1,0:T(2,128)(2,1)}), bf16[32,2,576]{2,1,0:T(2,128)(2,1)S(1)}, u32[]{:S(2)}, u32[]{:S(2)}) async-start(bf16[32,2,576]{2,1,0:T(2,128)(2,1)} %reshape.508), calls=%async_computation.3 | async-start | bytes 163840 | tf_op jit(solution)/shard_map/all_to_all | solution.py:54
  121.1 23.2 %collective-permute-start = (bf16[3,64,1,128]{3,1,0,2:T(8,128)(2,1)S(1)}, bf16[3,64,1,128]{3,1,0,2:T(8,128)(2,1)S(1)}, u32[]{:S(2)}, u32[]{:S(2)}) collective-permute-start(bf16[3,64,1,128]{3,1,0,2:T(8,128)(2,1)S(1)} %get-tuple-element.18), channel_id=1, source_target_pairs={{0,288},{32,320},{64,352},{96,384},{128,416},{160,448},{192,480},{... | collective-permute-start | bytes 147464 | tf_op jit(solution)/shard_map/ppermute | solution.py:24
  129.2 16.4 %collective-permute-start.1 = (bf16[3,64,1,128]{3,1,0,2:T(8,128)(2,1)S(1)}, bf16[3,64,1,128]{3,1,0,2:T(8,128)(2,1)S(1)}, u32[]{:S(2)}, u32[]{:S(2)}) collective-permute-start(bf16[3,64,1,128]{3,1,0,2:T(8,128)(2,1)S(1)} %get-tuple-element.17), channel_id=1, source_target_pairs={{0,256},{32,288},{64,320},{96,352},{128,384},{160,416},{192,448},{... | collective-permute-start | bytes 147464 | tf_op jit(solution)/shard_map/ppermute | solution.py:24
  132.4 14.5 %collective-permute-start.2 = (bf16[3,64,1,128]{3,1,0,2:T(8,128)(2,1)S(1)}, bf16[3,64,1,128]{3,1,0,2:T(8,128)(2,1)S(1)}, u32[]{:S(2)}, u32[]{:S(2)}) collective-permute-start(bf16[3,64,1,128]{3,1,0,2:T(8,128)(2,1)S(1)} %get-tuple-element.16), channel_id=1, source_target_pairs={{0,224},{32,256},{64,288},{96,320},{128,352},{160,384},{192,416},{... | collective-permute-start | bytes 147464 | tf_op jit(solution)/shard_map/ppermute | solution.py:24
  133.8 14.5 %collective-permute-start.3 = (bf16[3,64,1,128]{3,1,0,2:T(8,128)(2,1)S(1)}, bf16[3,64,1,128]{3,1,0,2:T(8,128)(2,1)S(1)}, u32[]{:S(2)}, u32[]{:S(2)}) collective-permute-start(bf16[3,64,1,128]{3,1,0,2:T(8,128)(2,1)S(1)} %get-tuple-element.15), channel_id=1, source_target_pairs={{0,32},{32,64},{64,96},{96,128},{128,160},{160,192},{192,224},{224... | collective-permute-start | bytes 147464 | tf_op jit(solution)/shard_map/ppermute | solution.py:24
  138.7 9.6 %collective-permute-start.4 = (bf16[3,64,1,128]{3,1,0,2:T(8,128)(2,1)S(1)}, bf16[3,64,1,128]{3,1,0,2:T(8,128)(2,1)S(1)}, u32[]{:S(2)}, u32[]{:S(2)}) collective-permute-start(bf16[3,64,1,128]{3,1,0,2:T(8,128)(2,1)S(1)} %get-tuple-element.14), channel_id=1, source_target_pairs={{32,0},{64,32},{96,64},{128,96},{160,128},{192,160},{224,192},{256... | collective-permute-start | bytes 147464 | tf_op jit(solution)/shard_map/ppermute | solution.py:24
  144.3 10.2 %collective-permute-start.5 = (bf16[3,64,1,128]{3,1,0,2:T(8,128)(2,1)S(1)}, bf16[3,64,1,128]{3,1,0,2:T(8,128)(2,1)S(1)}, u32[]{:S(2)}, u32[]{:S(2)}) collective-permute-start(bf16[3,64,1,128]{3,1,0,2:T(8,128)(2,1)S(1)} %get-tuple-element.13), channel_id=1, source_target_pairs={{224,0},{256,32},{288,64},{320,96},{352,128},{384,160},{416,192},{... | collective-permute-start | bytes 147464 | tf_op jit(solution)/shard_map/ppermute | solution.py:24
  145.6 11.6 %collective-permute-start.6 = (bf16[3,64,1,128]{3,1,0,2:T(8,128)(2,1)S(1)}, bf16[3,64,1,128]{3,1,0,2:T(8,128)(2,1)S(1)}, u32[]{:S(2)}, u32[]{:S(2)}) collective-permute-start(bf16[3,64,1,128]{3,1,0,2:T(8,128)(2,1)S(1)} %get-tuple-element.12), channel_id=1, source_target_pairs={{256,0},{288,32},{320,64},{352,96},{384,128},{416,160},{448,192},{... | collective-permute-start | bytes 147464 | tf_op jit(solution)/shard_map/ppermute | solution.py:24
  147.0 12.5 %collective-permute-start.7 = (bf16[3,64,1,128]{3,1,0,2:T(8,128)(2,1)S(1)}, bf16[3,64,1,128]{3,1,0,2:T(8,128)(2,1)S(1)}, u32[]{:S(2)}, u32[]{:S(2)}) collective-permute-start(bf16[3,64,1,128]{3,1,0,2:T(8,128)(2,1)S(1)} %get-tuple-element.11), channel_id=1, source_target_pairs={{288,0},{320,32},{352,64},{384,96},{416,128},{448,160},{480,192},{... | collective-permute-start | bytes 147464 | tf_op jit(solution)/shard_map/ppermute | solution.py:24
  168.3 1.9 copy-start.4
  178.7 0.9 copy-start.1
  179.6 1.4 copy-start.3
  193.7 10.4 %copy-start.2 = (bf16[9,64,576]{2,1,0:T(8,128)(2,1)S(1)}, bf16[9,64,576]{2,1,0:T(8,128)(2,1)}, u32[]{:S(2)}) copy-start(bf16[9,64,576]{2,1,0:T(8,128)(2,1)} %copy-done.1) | copy-start | bytes 1990660
  202.2 1.9 copy-start
  202.5 25.4 %collective-permute-start.8 = (bf16[3,64,1,128]{3,1,0,2:T(8,128)(2,1)S(1)}, bf16[3,64,1,128]{3,1,0,2:T(8,128)(2,1)S(1)}, u32[]{:S(2)}, u32[]{:S(2)}) collective-permute-start(bf16[3,64,1,128]{3,1,0,2:T(8,128)(2,1)S(1)} %get-tuple-element.10), channel_id=1, source_target_pairs={{288,0},{320,32},{352,64},{384,96},{416,128},{448,160},{480,192},{... | collective-permute-start | bytes 147464 | tf_op jit(solution)/shard_map/ppermute | solution.py:24
  205.7 45.5 %all-to-all-start.4 = ((bf16[32,2,576]{2,1,0:T(2,128)(2,1)}), bf16[32,2,576]{2,1,0:T(2,128)(2,1)S(1)}, u32[]{:S(2)}, u32[]{:S(2)}) async-start(bf16[32,2,576]{2,1,0:T(2,128)(2,1)} %reshape.516), calls=%async_computation.4 | async-start | bytes 163840 | tf_op jit(solution)/shard_map/all_to_all | solution.py:120
  219.1 16.0 %collective-permute-start.9 = (bf16[3,64,1,128]{3,1,0,2:T(8,128)(2,1)S(1)}, bf16[3,64,1,128]{3,1,0,2:T(8,128)(2,1)S(1)}, u32[]{:S(2)}, u32[]{:S(2)}) collective-permute-start(bf16[3,64,1,128]{3,1,0,2:T(8,128)(2,1)S(1)} %get-tuple-element.9), channel_id=1, source_target_pairs={{256,0},{288,32},{320,64},{352,96},{384,128},{416,160},{448,192},{... | collective-permute-start | bytes 147464 | tf_op jit(solution)/shard_map/ppermute | solution.py:24
  220.4 21.5 %collective-permute-start.10 = (bf16[3,64,1,128]{3,1,0,2:T(8,128)(2,1)S(1)}, bf16[3,64,1,128]{3,1,0,2:T(8,128)(2,1)S(1)}, u32[]{:S(2)}, u32[]{:S(2)}) collective-permute-start(bf16[3,64,1,128]{3,1,0,2:T(8,128)(2,1)S(1)} %get-tuple-element.8), channel_id=1, source_target_pairs={{224,0},{256,32},{288,64},{320,96},{352,128},{384,160},{416,192},{... | collective-permute-start | bytes 147464 | tf_op jit(solution)/shard_map/ppermute | solution.py:24
  221.7 25.1 %collective-permute-start.11 = (bf16[3,64,1,128]{3,1,0,2:T(8,128)(2,1)S(1)}, bf16[3,64,1,128]{3,1,0,2:T(8,128)(2,1)S(1)}, u32[]{:S(2)}, u32[]{:S(2)}) collective-permute-start(bf16[3,64,1,128]{3,1,0,2:T(8,128)(2,1)S(1)} %get-tuple-element.7), channel_id=1, source_target_pairs={{32,0},{64,32},{96,64},{128,96},{160,128},{192,160},{224,192},{256... | collective-permute-start | bytes 147464 | tf_op jit(solution)/shard_map/ppermute | solution.py:24
  224.9 21.9 %collective-permute-start.12 = (bf16[3,64,1,128]{3,1,0,2:T(8,128)(2,1)S(1)}, bf16[3,64,1,128]{3,1,0,2:T(8,128)(2,1)S(1)}, u32[]{:S(2)}, u32[]{:S(2)}) collective-permute-start(bf16[3,64,1,128]{3,1,0,2:T(8,128)(2,1)S(1)} %get-tuple-element.6), channel_id=1, source_target_pairs={{0,32},{32,64},{64,96},{96,128},{128,160},{160,192},{192,224},{224... | collective-permute-start | bytes 147464 | tf_op jit(solution)/shard_map/ppermute | solution.py:24
  227.9 19.0 %collective-permute-start.13 = (bf16[3,64,1,128]{3,1,0,2:T(8,128)(2,1)S(1)}, bf16[3,64,1,128]{3,1,0,2:T(8,128)(2,1)S(1)}, u32[]{:S(2)}, u32[]{:S(2)}) collective-permute-start(bf16[3,64,1,128]{3,1,0,2:T(8,128)(2,1)S(1)} %get-tuple-element.5), channel_id=1, source_target_pairs={{0,224},{32,256},{64,288},{96,320},{128,352},{160,384},{192,416},{... | collective-permute-start | bytes 147464 | tf_op jit(solution)/shard_map/ppermute | solution.py:24
  235.1 11.8 %collective-permute-start.14 = (bf16[3,64,1,128]{3,1,0,2:T(8,128)(2,1)S(1)}, bf16[3,64,1,128]{3,1,0,2:T(8,128)(2,1)S(1)}, u32[]{:S(2)}, u32[]{:S(2)}) collective-permute-start(bf16[3,64,1,128]{3,1,0,2:T(8,128)(2,1)S(1)} %get-tuple-element.4), channel_id=1, source_target_pairs={{0,256},{32,288},{64,320},{96,352},{128,384},{160,416},{192,448},{... | collective-permute-start | bytes 147464 | tf_op jit(solution)/shard_map/ppermute | solution.py:24
  241.9 6.1 %collective-permute-start.15 = (bf16[3,64,1,128]{3,1,0,2:T(8,128)(2,1)S(1)}, bf16[3,64,1,128]{3,1,0,2:T(8,128)(2,1)S(1)}, u32[]{:S(2)}, u32[]{:S(2)}) collective-permute-start(bf16[3,64,1,128]{3,1,0,2:T(8,128)(2,1)S(1)} %get-tuple-element.3), channel_id=1, source_target_pairs={{0,288},{32,320},{64,352},{96,384},{128,416},{160,448},{192,480},{... | collective-permute-start | bytes 147464 | tf_op jit(solution)/shard_map/ppermute | solution.py:24
  251.2 48.0 %all-to-all-start.5 = ((bf16[32,2,576]{2,1,0:T(2,128)(2,1)}), bf16[32,2,576]{2,1,0:T(2,128)(2,1)S(1)}, u32[]{:S(2)}, u32[]{:S(2)}) async-start(bf16[32,2,576]{2,1,0:T(2,128)(2,1)} %reshape.518), calls=%async_computation.5 | async-start | bytes 163840 | tf_op jit(solution)/shard_map/all_to_all | solution.py:121
  299.2 28.3 %all-to-all-start.6 = ((bf16[32,2,576]{2,1,0:T(2,128)(2,1)}), bf16[32,2,576]{2,1,0:T(2,128)(2,1)S(1)}, u32[]{:S(2)}, u32[]{:S(2)}) async-start(bf16[32,2,576]{2,1,0:T(2,128)(2,1)} %reshape.520), calls=%async_computation.6 | async-start | bytes 163840 | tf_op jit(solution)/shard_map/all_to_all | solution.py:122
where the time goes:
time: 334 us; the launch traced here: 329 us
  starting transfers between devices  135 us (40%)
  waiting for transfers between devices  127 us (38%)
  local copies, waits for them, and re-layouts  41.9 us (13%)
  other arithmetic  16 us (5%)
  matrix products  7.38 us (2%)
    ppermute x16, starting transfers between devices, from_behind(): lax.ppermute(value, axis, [(source, source + steps) for source in range(f...  52.6 us
    all_to_all x1, starting transfers between devices, per_device(): lax.all_to_all(queries, 'head', split_axis=1, concat_axis=0, tiled=True)  29.3 us
    all_to_all x1, waiting for transfers between devices, per_device(): lax.all_to_all(grad_k_loc, 'head', split_axis=0, concat_axis=1, tiled=True)  25.7 us
    all_to_all x1, waiting for transfers between devices, per_device(): lax.all_to_all(values_in, 'head', split_axis=1, concat_axis=0, tiled=True)  24.3 us
    all_to_all x1, waiting for transfers between devices, per_device(): lax.all_to_all(keys_in, 'head', split_axis=1, concat_axis=0, tiled=True)  23.4 us
    all_to_all x1, waiting for transfers between devices, per_device(): lax.all_to_all(grad_v_loc, 'head', split_axis=0, concat_axis=1, tiled=True)  22.5 us
    all_to_all x1, starting transfers between devices, per_device(): lax.all_to_all(grad_k_loc, 'head', split_axis=0, concat_axis=1, tiled=True)  21.5 us
    all_to_all x1, waiting for transfers between devices, per_device(): lax.all_to_all(queries, 'head', split_axis=1, concat_axis=0, tiled=True)  15.5 us
  transfers between devices with their start and end apart: 23, of which 10 were waited for; matrix products, arithmetic and copies ran while one was open for 5% of the time, Pallas kernels for 0%

commit v1 on v0

v1 whole, which is shorter than its diff:
```python
import functools

import jax
import jax.numpy as jnp
from jax import lax
from jax.experimental import pallas as pl
from jax.experimental.pallas import tpu as pltpu
from jax.sharding import PartitionSpec as P

HD = 64
LANES = 128
PATCH = 8
BT = 64
GRID_ROWS = 4
DIRS = 8
WIN = 9
QB_DOM = 9
CAP = 3
MAIN = 16
SLOTS = QB_DOM + DIRS * CAP
OFFSETS = [(-1, -1), (-1, 0), (-1, 1), (0, -1), (0, 1), (1, -1), (1, 0), (1, 1)]
MESH = pl.DeviceIdType.MESH
F32 = jnp.float32
BF16 = jnp.bfloat16


def live_slots(row_step, col_step):
    return 1 if row_step and col_step else CAP


def turn_matrix(orient_id):
    token = lax.broadcasted_iota(jnp.int32, (BT, BT), 0)
    target = lax.broadcasted_iota(jnp.int32, (BT, BT), 1)
    r = lax.shift_right_logical(token, 3)
    s = lax.bitwise_and(token, 7)
    flip_r = lax.bitwise_and(orient_id, 1)
    flip_s = lax.bitwise_and(lax.shift_right_logical(orient_id, 1), 1)
    swap = lax.bitwise_and(lax.shift_right_logical(orient_id, 2), 1)
    r2 = r + flip_r * (PATCH - 1 - 2 * r)
    s2 = s + flip_s * (PATCH - 1 - 2 * s)
    mapped = swap * (PATCH * s2 + r2) + (1 - swap) * (PATCH * r2 + s2)
    return jnp.where(target == mapped, 1.0, 0.0).astype(BF16)


def kernel(
    heads, doms,
    near_ref, send_ref, orient_ref, q_ref, k_ref, v_ref, g_ref, bias_ref,
    gq_ref, gk_ref, gv_ref,
    main_out, rest_out, main_in, rest_in,
    pair_rows, qg_rows, ext, staged, arrived, turns,
    window_grads, gq_rows, total_rows, leaving, returned,
    a_out, b_out, c_out, a_in, b_in, c_in,
    inv_near, inv_send,
    in_send, in_recv, dom_send, dom_recv, back_send, back_recv, out_send, out_recv,
):
    grid_cols = doms // GRID_ROWS
    peers = heads - 1
    me = lax.axis_index("head")
    dom = lax.axis_index("dom")
    row = dom // grid_cols
    col = dom % grid_cols
    scale = HD ** (-0.5)

    def inside(r, c):
        return (r >= 0) & (r < GRID_ROWS) & (c >= 0) & (c < grid_cols)

    lender_ok = [inside(row + dr, col + dc) for dr, dc in OFFSETS]
    borrower_ok = [inside(row - dr, col - dc) for dr, dc in OFFSETS]
    lender = [dom + dr * grid_cols + dc for dr, dc in OFFSETS]
    borrower = [dom - dr * grid_cols - dc for dr, dc in OFFSETS]

    def peer_of(n):
        half = (n + 1) // 2
        off = heads // 2 + half * (1 - 2 * (n % 2))
        return (me + off) % heads

    window_grads[:, WIN] = jnp.zeros((QB_DOM, BT, LANES), F32)
    returned[:, CAP] = jnp.zeros((DIRS, BT, LANES), BF16)

    barrier = pltpu.get_barrier_semaphore()

    @pl.loop(0, peers)
    def _(n):
        pl.semaphore_signal(barrier, inc=1, device_id={"head": peer_of(n)}, device_id_type=MESH)

    near_count = jnp.int32(0)
    for kk in range(DIRS):
        near_count = near_count + lender_ok[kk].astype(jnp.int32)

        @pl.when(lender_ok[kk])
        def _():
            pl.semaphore_signal(barrier, inc=1, device_id={"dom": lender[kk]}, device_id_type=MESH)

    def left_half(rows):
        return lax.broadcasted_iota(jnp.int32, (rows, LANES), 1) < HD

    def swap_halves(x):
        return pltpu.roll(x, HD, 1)

    def merge(x, y):
        mask = left_half(x.shape[0])
        return jnp.where(mask, x, swap_halves(y)), jnp.where(mask, swap_halves(x), y)

    @pl.loop(0, heads // 2)
    def _(i):
        cols = pl.ds(pl.multiple_of(i * LANES, LANES), LANES)
        for part, (first, second) in enumerate(((k_ref, v_ref), (q_ref, g_ref))):
            x, y = first[0:MAIN, cols].astype(F32), second[0:MAIN, cols].astype(F32)
            even, odd = merge(x, y)
            main_out[part, 2 * i] = even.astype(BF16)
            main_out[part, 2 * i + 1] = odd.astype(BF16)
            x, y = first[MAIN:, cols].astype(F32), second[MAIN:, cols].astype(F32)
            even, odd = merge(x, y)
            rest_out[part, 2 * i] = even.astype(BF16)
            rest_out[part, 2 * i + 1] = odd.astype(BF16)

    def lent_block(kk, c):
        if live_slots(*OFFSETS[kk]) == CAP:
            return send_ref[0, kk, c]
        return jnp.maximum(jnp.maximum(send_ref[0, kk, 0], send_ref[0, kk, 1]), send_ref[0, kk, 2])

    @pl.loop(0, QB_DOM)
    def _(b):
        names = [near_ref[b, j] for j in range(WIN)]

        def place(first, last):
            at = jnp.int32(WIN)
            for j in range(WIN):
                at = jnp.where((names[j] >= first) & (names[j] <= last), j, at)
            return at

        for e in range(QB_DOM):
            inv_near[b, e] = place(e, e)
        for kk, step in enumerate(OFFSETS):
            live = live_slots(*step)
            for c in range(live):
                e = QB_DOM + kk * CAP + c
                inv_near[b, e] = place(e, e + CAP - live)
        for kk, step in enumerate(OFFSETS):
            at = jnp.int32(CAP)
            for c in range(live_slots(*step)):
                at = jnp.where(borrower_ok[kk] & (lent_block(kk, c) == b), c, at)
            inv_send[b, kk] = at

    for kk in range(DIRS):
        turns[kk] = turn_matrix(orient_ref[0, kk])

    pl.semaphore_wait(barrier, peers + near_count)

    def to_peer(src, dst, sem, peer):
        return pltpu.make_async_remote_copy(
            src_ref=src, dst_ref=dst, send_sem=in_send.at[sem], recv_sem=in_recv.at[sem],
            device_id={"head": peer}, device_id_type=MESH,
        )

    for part in range(2):

        @pl.loop(0, peers)
        def _(n):
            peer = peer_of(n)
            to_peer(main_out.at[part, peer], main_in.at[part, me], 2 * part, peer).start()
            to_peer(rest_out.at[part, peer], rest_in.at[part, me], 2 * part + 1, peer).start()

        main_in[part, me] = main_out[part, me]
        rest_in[part, me] = rest_out[part, me]

    some = pl.ds(0, peers)

    def unpack_rows(part, rows):
        to_peer(main_out.at[part, some], main_in.at[part, some], 2 * part, peer_of(0)).wait_recv()
        to_peer(rest_out.at[part, some], rest_in.at[part, some], 2 * part + 1, peer_of(0)).wait_recv()
        count = MAIN + rest_in.shape[2]
        for source in range(heads):
            base = source * count
            rows[base:base + MAIN] = main_in[part, source].astype(F32)
            rows[base + MAIN:base + count] = rest_in[part, source].astype(F32)

    unpack_rows(0, pair_rows)
    for b in range(QB_DOM):
        ext[b] = pair_rows[b * BT:(b + 1) * BT].astype(BF16)

    def lend(kk):
        live = pl.ds(0, live_slots(*OFFSETS[kk]))
        return pltpu.make_async_remote_copy(
            src_ref=staged.at[kk, live], dst_ref=arrived.at[kk, live],
            send_sem=dom_send.at[kk], recv_sem=dom_recv.at[kk],
            device_id={"dom": borrower[kk]}, device_id_type=MESH,
        )

    for kk, step in enumerate(OFFSETS):
        for c in range(live_slots(*step)):
            staged[kk, c] = ext[lent_block(kk, c)]
    for kk in range(DIRS):

        @pl.when(borrower_ok[kk])
        def _():
            lend(kk).start()

    unpack_rows(1, qg_rows)

    for kk, step in enumerate(OFFSETS):

        @pl.when(lender_ok[kk])
        def _():
            lend(kk).wait_recv()
            for c in range(live_slots(*step)):
                turned = jnp.dot(turns[kk], arrived[kk, c], preferred_element_type=F32).astype(BF16)
                for same in range(c, c + 1 + CAP - live_slots(*step)):
                    ext[QB_DOM + kk * CAP + same] = turned

    lane = lax.broadcasted_iota(jnp.int32, (1, LANES), 1)
    pair_scale = jnp.where(lane < HD, scale, 1.0).astype(F32)

    @pl.loop(0, QB_DOM)
    def _(b):
        rows = pl.ds(pl.multiple_of(b * BT, BT), BT)
        qg = qg_rows[rows]
        mask = left_half(BT)
        qg2 = jnp.concatenate([jnp.where(mask, qg, 0.0), jnp.where(mask, 0.0, qg)], axis=0).astype(BF16)
        window = jnp.concatenate([ext[near_ref[b, j]] for j in range(WIN)], axis=0)
        both = lax.dot_general(qg2, window, (((1,), (1,)), ((), ())), preferred_element_type=F32)
        scores = both[:BT] * scale + bias_ref[0]
        dprobs = both[BT:]
        top = jnp.max(scores, axis=1, keepdims=True)
        exps = jnp.exp(scores - top)
        probs = exps / jnp.sum(exps, axis=1, keepdims=True)
        half = probs.astype(BF16)
        delta = jnp.sum(half.astype(F32) * dprobs, axis=1, keepdims=True)
        dscores = (probs * (dprobs - delta)).astype(BF16)
        gq_rows[rows] = jnp.dot(dscores, window, preferred_element_type=F32) * scale
        stacked = jnp.concatenate([dscores, half], axis=0)
        grads = lax.dot_general(stacked, qg2, (((0,), (0,)), ((), ())), preferred_element_type=F32)
        grads = grads * pair_scale
        for j in range(WIN):
            window_grads[b, j] = grads[j * BT:(j + 1) * BT]

    def slot_grad(e):
        acc = window_grads[0, inv_near[0, e]]
        for b in range(1, QB_DOM):
            acc = acc + window_grads[b, inv_near[b, e]]
        return acc

    def give_back(kk):
        live = pl.ds(0, live_slots(*OFFSETS[kk]))
        return pltpu.make_async_remote_copy(
            src_ref=leaving.at[kk, live], dst_ref=returned.at[kk, live],
            send_sem=back_send.at[kk], recv_sem=back_recv.at[kk],
            device_id={"dom": lender[kk]}, device_id_type=MESH,
        )

    for kk, step in enumerate(OFFSETS):

        @pl.when(lender_ok[kk])
        def _():
            for c in range(live_slots(*step)):
                leaving[kk, c] = lax.dot_general(
                    turns[kk], slot_grad(QB_DOM + kk * CAP + c).astype(BF16),
                    (((0,), (0,)), ((), ())), preferred_element_type=F32,
                ).astype(BF16)

    for kk in range(DIRS):

        @pl.when(lender_ok[kk])
        def _():
            give_back(kk).start()

    def home(src, dst, sem, peer):
        return pltpu.make_async_remote_copy(
            src_ref=src, dst_ref=dst, send_sem=out_send.at[sem], recv_sem=out_recv.at[sem],
            device_id={"head": peer}, device_id_type=MESH,
        )

    count = MAIN + rest_in.shape[2]
    half_main = MAIN // 2
    for peer in range(heads):
        base = peer * count
        first = gq_rows[base:base + half_main]
        second = gq_rows[base + half_main:base + MAIN]
        a_out[peer] = jnp.where(left_half(half_main), first, swap_halves(second)).astype(BF16)

    @pl.loop(0, peers)
    def _(n):
        peer = peer_of(n)
        home(a_out.at[peer], a_in.at[me], 0, peer).start()

    a_in[me] = a_out[me]

    for b in range(QB_DOM):
        total_rows[b * BT:(b + 1) * BT] = slot_grad(b)

    for kk in range(DIRS):

        @pl.when(borrower_ok[kk])
        def _():
            give_back(kk).wait_recv()

    for b in range(QB_DOM):
        acc = total_rows[b * BT:(b + 1) * BT]
        for kk in range(DIRS):
            acc = acc + returned[kk, inv_send[b, kk]].astype(F32)
        total_rows[b * BT:(b + 1) * BT] = acc

    for peer in range(heads):
        base = peer * count
        b_out[peer] = total_rows[base:base + MAIN].astype(BF16)
        rest = total_rows[base + MAIN:base + count]
        c_out[peer, 0:2] = rest.astype(BF16)
        rest = gq_rows[base + MAIN:base + count]
        c_out[peer, 2:4] = rest.astype(BF16)

    @pl.loop(0, peers)
    def _(n):
        peer = peer_of(n)
        home(b_out.at[peer], b_in.at[me], 1, peer).start()
        home(c_out.at[peer], c_in.at[me], 2, peer).start()

    b_in[me] = b_out[me]
    c_in[me] = c_out[me]

    home(a_out.at[some], a_in.at[some], 0, peer_of(0)).wait_recv()
    home(b_out.at[some], b_in.at[some], 1, peer_of(0)).wait_recv()
    home(c_out.at[some], c_in.at[some], 2, peer_of(0)).wait_recv()

    @pl.loop(0, heads // 2)
    def _(i):
        cols = pl.ds(pl.multiple_of(i * LANES, LANES), LANES)
        x, y = a_in[2 * i].astype(F32), a_in[2 * i + 1].astype(F32)
        mask = left_half(half_main)
        gq_ref[0:half_main, cols] = jnp.where(mask, x, swap_halves(y)).astype(BF16)
        gq_ref[half_main:MAIN, cols] = jnp.where(mask, swap_halves(x), y).astype(BF16)
        x, y = b_in[2 * i].astype(F32), b_in[2 * i + 1].astype(F32)
        mask = left_half(MAIN)
        gk_ref[0:MAIN, cols] = jnp.where(mask, x, swap_halves(y)).astype(BF16)
        gv_ref[0:MAIN, cols] = jnp.where(mask, swap_halves(x), y).astype(BF16)
        x, y = c_in[2 * i].astype(F32), c_in[2 * i + 1].astype(F32)
        mask = left_half(4)
        front = jnp.where(mask, x, swap_halves(y))
        gk_ref[MAIN:count, cols] = front[0:2].astype(BF16)
        gq_ref[MAIN:count, cols] = front[2:4].astype(BF16)
        back = jnp.where(mask, swap_halves(x), y)
        gv_ref[MAIN:count, cols] = back[0:2].astype(BF16)

    for part in range(2):
        to_peer(main_out.at[part, some], main_in.at[part, some], 2 * part, peer_of(0)).wait_send()
        to_peer(rest_out.at[part, some], rest_in.at[part, some], 2 * part + 1, peer_of(0)).wait_send()
    for kk in range(DIRS):

        @pl.when(borrower_ok[kk])
        def _():
            lend(kk).wait_send()

        @pl.when(lender_ok[kk])
        def _():
            give_back(kk).wait_send()

    home(a_out.at[some], a_in.at[some], 0, peer_of(0)).wait_send()
    home(b_out.at[some], b_in.at[some], 1, peer_of(0)).wait_send()
    home(c_out.at[some], c_in.at[some], 2, peer_of(0)).wait_send()


def per_device(heads, doms, queries, keys_in, values_in, grad_out, pos_bias, neighbours, send_block, orient):
    rows, width = queries.shape
    rest = rows - MAIN
    tokens = QB_DOM * BT
    whole = pl.BlockSpec(memory_space=pltpu.VMEM)
    small = pl.BlockSpec(memory_space=pltpu.SMEM)
    out = jax.ShapeDtypeStruct((rows, width), BF16)
    block = (BT, LANES)
    dma = pltpu.SemaphoreType.DMA
    return pl.pallas_call(
        functools.partial(kernel, heads, doms),
        out_shape=(out, out, out),
        in_specs=[small] * 3 + [whole] * 5,
        out_specs=(whole, whole, whole),
        scratch_shapes=[
            pltpu.VMEM((2, heads, MAIN, LANES), BF16),
            pltpu.VMEM((2, heads, rest, LANES), BF16),
            pltpu.VMEM((2, heads, MAIN, LANES), BF16),
            pltpu.VMEM((2, heads, rest, LANES), BF16),
            pltpu.VMEM((tokens, LANES), F32),
            pltpu.VMEM((tokens, LANES), F32),
            pltpu.VMEM((SLOTS,) + block, BF16),
            pltpu.VMEM((DIRS, CAP) + block, BF16),
            pltpu.VMEM((DIRS, CAP) + block, BF16),
            pltpu.VMEM((DIRS, BT, BT), BF16),
            pltpu.VMEM((QB_DOM, WIN + 1) + block, F32),
            pltpu.VMEM((tokens, LANES), F32),
            pltpu.VMEM((tokens, LANES), F32),
            pltpu.VMEM((DIRS, CAP) + block, BF16),
            pltpu.VMEM((DIRS, CAP + 1) + block, BF16),
            pltpu.VMEM((heads, MAIN // 2, LANES), BF16),
            pltpu.VMEM((heads, MAIN, LANES), BF16),
            pltpu.VMEM((heads, 2 * rest, LANES), BF16),
            pltpu.VMEM((heads, MAIN // 2, LANES), BF16),
            pltpu.VMEM((heads, MAIN, LANES), BF16),
            pltpu.VMEM((heads, 2 * rest, LANES), BF16),
            pltpu.SMEM((QB_DOM, SLOTS), jnp.int32),
            pltpu.SMEM((QB_DOM, DIRS), jnp.int32),
            dma((4,)), dma((4,)),
            dma((DIRS,)), dma((DIRS,)),
            dma((DIRS,)), dma((DIRS,)),
            dma((3,)), dma((3,)),
        ],
        compiler_params=pltpu.CompilerParams(collective_id=0, has_side_effects=True),
    )(neighbours, send_block, orient, queries, keys_in, values_in, grad_out, pos_bias)


def solution(mesh):
    both = P(("dom", "head"), None)
    return jax.shard_map(
        functools.partial(per_device, mesh.shape["head"], mesh.shape["dom"]),
        mesh=mesh,
        in_specs=(both, both, both, both, P("head", None, None), P("dom", None), P("dom", None, None), P("dom", None)),
        out_specs=(both, both, both),
        check_vma=False,
    )
```

time: 334 us -> 98.7 us (0.30); the launches traced: 329 us -> 97.7 us
  starting transfers between devices: 135 us -> 0 us
  waiting for transfers between devices: 127 us -> 0 us
  Pallas kernels: 0 us -> 92.6 us
  local copies, waits for them, and re-layouts: 41.9 us -> 4.49 us
  other arithmetic: 16 us -> 0 us
  matrix products: 7.38 us -> 0 us
    all_to_all x7 -> x0, waiting for transfers between devices: 115 us -> none  [the longest x1 25.7 us: per_device(): lax.all_to_all(grad_k_loc, 'head', split_axis=0, concat_axis=1, tiled=True)]
    pallas_call x0 -> x1, Pallas kernels: none -> 92.6 us  [per_device(): pl.pallas_call(functools.partial(kernel, heads, doms), out_shape=(out, ou...]
    all_to_all x7 -> x0, starting transfers between devices: 82.4 us -> none  [the longest x1 29.3 us: per_device(): lax.all_to_all(queries, 'head', split_axis=1, concat_axis=0, tiled=True)]
    ppermute x16 -> x0, starting transfers between devices: 52.6 us -> none  [from_behind(): lax.ppermute(value, axis, [(source, source + steps) for source in range(f...]
    gather x8 -> x0, local copies, waits for them, and re-layouts: 22.1 us -> none  [the longest x2 8.54 us: per_device(): jnp.take_along_axis(arrived, turn_index[:, :, None, None], axis=1)]
    ppermute x16 -> x0, waiting for transfers between devices: 12.1 us -> none  [from_behind(): lax.ppermute(value, axis, [(source, source + steps) for source in range(f...]
    scatter-add x2 -> x0, other arithmetic: 12.1 us -> none  [the longest x1 9.98 us: per_device(): jax.ops.segment_sum(window_grad, near_ids, num_segments=slot_total)]
    dot_general x5 -> x0, matrix products: 7.38 us -> none  [the longest x1 2.41 us: per_device(): jnp.einsum('bhtk,bthd->bkhd', probs_half, grad_blk, preferred_element_typ...]
  transfers between devices with their start and end apart: 23 -> 0, of which waited for: 10 -> 0; matrix products, arithmetic and copies ran while one was open for 5% -> 0% of each run, Pallas kernels for 0% -> 0%
where the time goes in v1:
time: 98.7 us; the launch traced here: 97.7 us
  Pallas kernels  92.6 us (94%)
  local copies, waits for them, and re-layouts  4.49 us (5%)
    pallas_call x1, Pallas kernels, per_device(): pl.pallas_call(functools.partial(kernel, heads, doms), out_shape=(out, ou...  92.6 us
    unnamed x8, local copies, waits for them, and re-layouts  4.49 us

profile of v1, /device:TPU:1, one launch (start us, length us, event | category | flops | bytes accessed | tf_op | source)
XLA Modules:
  0.0 97.7 jit_solution(1822787982792319906)
XLA Ops:
  0.6 1.3 %copy.11.send_ref = s32[1,8,3]{2,1,0:T(8,128)} copy(s32[1,8,3]{1,0,2:T(1,128)} %param.14) | data formatting | bytes 192 | tf_op args[6]
  2.0 92.6 %shard_map.103 = (bf16[18,2048]{1,0:T(8,128)(2,1)}, bf16[18,2048]{1,0:T(8,128)(2,1)}, bf16[18,2048]{1,0:T(8,128)(2,1)}) custom-call(s32[9,9]{1,0:T(8,128)} %near_ref.1, s32[1,8,3]{2,1,0:T(8,128)} %copy.11.send_ref, s32[1,8]{1,0:T(1,128)} %orient_ref.1, bf16[18,2048]{1,0:T(8,128)(2,1)} %q_ref.1, bf16[18,2048]{1,0:T(8,128)(2,1)} %k_ref.1, ...), custom_call_target="tpu_custom_call" | custom-call | tf_op jit(solution)/shard_map/pallas_call | solution.py:370
  94.5 0.0 copy-start.1
  94.6 1.6 %copy.15 = bf16[18,2048]{1,0:T(8,128)(2,1)} copy(bf16[18,2048]{1,0:T(8,128)(2,1)} %get-tuple-element.6) | data formatting | bytes 147456
  96.1 0.0 copy-done.1
  96.1 0.0 copy-start
  96.1 0.6 copy.16
  96.8 0.3 copy-done
  97.1 0.6 copy.17
Async XLA Ops:
  94.5 1.6 %copy-start.1 = (bf16[18,2048]{1,0:T(8,128)(2,1)S(1)}, bf16[18,2048]{1,0:T(8,128)(2,1)}, u32[]{:S(2)}) copy-start(bf16[18,2048]{1,0:T(8,128)(2,1)} %get-tuple-element.7) | copy-start | bytes 221188
  96.1 0.9 copy-start

commit v2 on v1

--- a/solution.py
+++ b/solution.py
@@ -44,13 +44,15 @@
 
 def kernel(
     heads, doms,
-    near_ref, send_ref, orient_ref, q_ref, k_ref, v_ref, g_ref, bias_ref,
+    near_ref, send_ref, orient_ref, q_any, k_any, v_any, g_any, bias_any,
     gq_ref, gk_ref, gv_ref,
+    q_ref, k_ref, v_ref, g_ref, bias_ref,
     main_out, rest_out, main_in, rest_in,
     pair_rows, qg_rows, ext, staged, arrived, turns,
     window_grads, gq_rows, total_rows, leaving, returned,
     a_out, b_out, c_out, a_in, b_in, c_in,
     inv_near, inv_send,
+    load_sem, right_sem, left_sem,
     in_send, in_recv, dom_send, dom_recv, back_send, back_recv, out_send, out_recv,
 ):
     grid_cols = doms // GRID_ROWS
@@ -74,22 +76,26 @@
         off = heads // 2 + half * (1 - 2 * (n % 2))
         return (me + off) % heads
 
-    window_grads[:, WIN] = jnp.zeros((QB_DOM, BT, LANES), F32)
+    right, left = (me + 1) % heads, (me + peers) % heads
+    far = heads // 2
+
     returned[:, CAP] = jnp.zeros((DIRS, BT, LANES), BF16)
 
     barrier = pltpu.get_barrier_semaphore()
-
-    @pl.loop(0, peers)
-    def _(n):
-        pl.semaphore_signal(barrier, inc=1, device_id={"head": peer_of(n)}, device_id_type=MESH)
-
-    near_count = jnp.int32(0)
+    near_count = jnp.int32(2)
+    for side in (right, left):
+        pl.semaphore_signal(barrier, inc=1, device_id={"head": side}, device_id_type=MESH)
     for kk in range(DIRS):
         near_count = near_count + lender_ok[kk].astype(jnp.int32)
 
         @pl.when(lender_ok[kk])
         def _():
             pl.semaphore_signal(barrier, inc=1, device_id={"dom": lender[kk]}, device_id_type=MESH)
+
+    pairs = ((k_any, k_ref), (v_any, v_ref), (q_any, q_ref), (g_any, g_ref), (bias_any, bias_ref))
+    loads = [pltpu.make_async_copy(src, dst, load_sem.at[n]) for n, (src, dst) in enumerate(pairs)]
+    for load in loads:
+        load.start()
 
     def left_half(rows):
         return lax.broadcasted_iota(jnp.int32, (rows, LANES), 1) < HD
@@ -101,10 +107,9 @@
         mask = left_half(x.shape[0])
         return jnp.where(mask, x, swap_halves(y)), jnp.where(mask, swap_halves(x), y)
 
-    @pl.loop(0, heads // 2)
-    def _(i):
-        cols = pl.ds(pl.multiple_of(i * LANES, LANES), LANES)
-        for part, (first, second) in enumerate(((k_ref, v_ref), (q_ref, g_ref))):
+    def pack(part, first, second):
+        for i in range(heads // 2):
+            cols = slice(i * LANES, (i + 1) * LANES)
             x, y = first[0:MAIN, cols].astype(F32), second[0:MAIN, cols].astype(F32)
             even, odd = merge(x, y)
             main_out[part, 2 * i] = even.astype(BF16)
@@ -113,11 +118,60 @@
             even, odd = merge(x, y)
             rest_out[part, 2 * i] = even.astype(BF16)
             rest_out[part, 2 * i + 1] = odd.astype(BF16)
+        main_in[part, me] = main_out[part, me]
+        rest_in[part, me] = rest_out[part, me]
+
+    def to_peer(src, dst, sem, peer):
+        return pltpu.make_async_remote_copy(
+            src_ref=src, dst_ref=dst, send_sem=in_send.at[sem], recv_sem=in_recv.at[sem],
+            device_id={"head": peer}, device_id_type=MESH,
+        )
+
+    def send_rows(part, peer):
+        to_peer(main_out.at[part, peer], main_in.at[part, me], 2 * part, peer).start()
+        to_peer(rest_out.at[part, peer], rest_in.at[part, me], 2 * part + 1, peer).start()
+
+    loads[0].wait()
+    loads[1].wait()
+    pack(0, k_ref, v_ref)
+
+    pl.semaphore_wait(barrier, near_count)
+
+    def pass_on(m):
+        pl.semaphore_signal(right_sem.at[m + 1], inc=1, device_id={"head": left}, device_id_type=MESH)
+
+        @pl.when(m + 1 < far)
+        def _():
+            pl.semaphore_signal(left_sem.at[m + 1], inc=1, device_id={"head": right}, device_id_type=MESH)
+
+    pass_on(1)
+    send_rows(0, right)
+    send_rows(0, left)
+
+    @pl.loop(2, far)
+    def _(m):
+        pl.semaphore_wait(right_sem.at[m], 1)
+        pl.semaphore_wait(left_sem.at[m], 1)
+        pass_on(m)
+        send_rows(0, (me + m) % heads)
+        send_rows(0, (me + heads - m) % heads)
+
+    loads[2].wait()
+    loads[3].wait()
+    pack(1, q_ref, g_ref)
+    pl.semaphore_wait(right_sem.at[far], 1)
+    send_rows(0, (me + far) % heads)
+
+    @pl.loop(0, peers)
+    def _(n):
+        send_rows(1, peer_of(n))
+
+    window_grads[:, WIN] = jnp.zeros((QB_DOM, BT, LANES), F32)
 
     def lent_block(kk, c):
         if live_slots(*OFFSETS[kk]) == CAP:
-            return send_ref[0, kk, c]
-        return jnp.maximum(jnp.maximum(send_ref[0, kk, 0], send_ref[0, kk, 1]), send_ref[0, kk, 2])
+            return send_ref[c, 0, kk]
+        return jnp.maximum(jnp.maximum(send_ref[0, 0, kk], send_ref[1, 0, kk]), send_ref[2, 0, kk])
 
     @pl.loop(0, QB_DOM)
     def _(b):
@@ -145,25 +199,6 @@
     for kk in range(DIRS):
         turns[kk] = turn_matrix(orient_ref[0, kk])
 
-    pl.semaphore_wait(barrier, peers + near_count)
-
-    def to_peer(src, dst, sem, peer):
-        return pltpu.make_async_remote_copy(
-            src_ref=src, dst_ref=dst, send_sem=in_send.at[sem], recv_sem=in_recv.at[sem],
-            device_id={"head": peer}, device_id_type=MESH,
-        )
-
-    for part in range(2):
-
-        @pl.loop(0, peers)
-        def _(n):
-            peer = peer_of(n)
-            to_peer(main_out.at[part, peer], main_in.at[part, me], 2 * part, peer).start()
-            to_peer(rest_out.at[part, peer], rest_in.at[part, me], 2 * part + 1, peer).start()
-
-        main_in[part, me] = main_out[part, me]
-        rest_in[part, me] = rest_out[part, me]
-
     some = pl.ds(0, peers)
 
     def unpack_rows(part, rows):
@@ -208,12 +243,12 @@
                 for same in range(c, c + 1 + CAP - live_slots(*step)):
                     ext[QB_DOM + kk * CAP + same] = turned
 
+    loads[4].wait()
     lane = lax.broadcasted_iota(jnp.int32, (1, LANES), 1)
     pair_scale = jnp.where(lane < HD, scale, 1.0).astype(F32)
 
-    @pl.loop(0, QB_DOM)
-    def _(b):
-        rows = pl.ds(pl.multiple_of(b * BT, BT), BT)
+    for b in range(QB_DOM):
+        rows = slice(b * BT, (b + 1) * BT)
         qg = qg_rows[rows]
         mask = left_half(BT)
         qg2 = jnp.concatenate([jnp.where(mask, qg, 0.0), jnp.where(mask, 0.0, qg)], axis=0).astype(BF16)
@@ -370,9 +405,11 @@
     return pl.pallas_call(
         functools.partial(kernel, heads, doms),
         out_shape=(out, out, out),
-        in_specs=[small] * 3 + [whole] * 5,
+        in_specs=[small] * 3 + [pl.BlockSpec(memory_space=pl.ANY)] * 5,
         out_specs=(whole, whole, whole),
         scratch_shapes=[
+            *[pltpu.VMEM((rows, width), BF16)] * 4,
+            pltpu.VMEM(pos_bias.shape, F32),
             pltpu.VMEM((2, heads, MAIN, LANES), BF16),
             pltpu.VMEM((2, heads, rest, LANES), BF16),
             pltpu.VMEM((2, heads, MAIN, LANES), BF16),
@@ -396,13 +433,16 @@
             pltpu.VMEM((heads, 2 * rest, LANES), BF16),
             pltpu.SMEM((QB_DOM, SLOTS), jnp.int32),
             pltpu.SMEM((QB_DOM, DIRS), jnp.int32),
+            dma((5,)),
+            pltpu.SemaphoreType.REGULAR((heads // 2 + 1,)),
+            pltpu.SemaphoreType.REGULAR((heads // 2 + 1,)),
             dma((4,)), dma((4,)),
             dma((DIRS,)), dma((DIRS,)),
             dma((DIRS,)), dma((DIRS,)),
             dma((3,)), dma((3,)),
         ],
         compiler_params=pltpu.CompilerParams(collective_id=0, has_side_effects=True),
-    )(neighbours, send_block, orient, queries, keys_in, values_in, grad_out, pos_bias)
+    )(neighbours, jnp.transpose(send_block, (2, 0, 1)), orient, queries, keys_in, values_in, grad_out, pos_bias)
 
 
 def solution(mesh):

time: 98.7 us -> 99.5 us (level)
  Pallas kernels: 92.6 us -> 94.6 us
  local copies, waits for them, and re-layouts: 4.49 us -> 3.15 us
    pallas_call x1, Pallas kernels: 92.6 us -> 94.6 us  [per_device(): pl.pallas_call(functools.partial(kernel, heads, doms), out_shape=(out, ou...]
    unnamed x8 -> x7, local copies, waits for them, and re-layouts: 4.49 us -> 3.15 us
where the time goes in v2:
time: 99.5 us; the launch traced here: 98.4 us
  Pallas kernels  94.6 us (95%)
  local copies, waits for them, and re-layouts  3.15 us (3%)
    pallas_call x1, Pallas kernels, per_device(): pl.pallas_call(functools.partial(kernel, heads, doms), out_shape=(out, ou...  94.6 us
    unnamed x7, local copies, waits for them, and re-layouts  3.15 us

profile of v2, /device:TPU:1, one launch (start us, length us, event | category | flops | bytes accessed | tf_op | source)
XLA Modules:
  0.0 98.4 jit_solution(16210007798623733249)
XLA Ops:
  0.6 94.6 %shard_map.103 = (bf16[18,2048]{1,0:T(8,128)(2,1)}, bf16[18,2048]{1,0:T(8,128)(2,1)}, bf16[18,2048]{1,0:T(8,128)(2,1)}) custom-call(s32[9,9]{1,0:T(8,128)} %near_ref.1, s32[3,1,8]{2,1,0:T(1,128)} %bitcast.1, s32[1,8]{1,0:T(1,128)} %orient_ref.1, bf16[18,2048]{1,0:T(8,128)(2,1)} %q_any.1, bf16[18,2048]{1,0:T(8,128)(2,1)} %k_any.1, bf16[18,2048]{1,0:T(8,128)(2,1)} %v_any.1, ...), custom_call_target="tpu_custom_call" | custom-call | tf_op jit(solution)/shard_map/pallas_call | solution.py:405
  95.2 0.0 copy-start.1
  95.2 1.6 %copy.14 = bf16[18,2048]{1,0:T(8,128)(2,1)} copy(bf16[18,2048]{1,0:T(8,128)(2,1)} %get-tuple-element.6) | data formatting | bytes 147456
  96.8 0.0 copy-done.1
  96.8 0.0 copy-start
  96.8 0.6 copy.15
  97.4 0.3 copy-done
  97.7 0.6 copy.16
Async XLA Ops:
  95.2 1.6 %copy-start.1 = (bf16[18,2048]{1,0:T(8,128)(2,1)S(1)}, bf16[18,2048]{1,0:T(8,128)(2,1)}, u32[]{:S(2)}) copy-start(bf16[18,2048]{1,0:T(8,128)(2,1)} %get-tuple-element.7) | copy-start | bytes 221188
  96.8 0.9 copy-start

commit v3 on v2

--- a/solution.py
+++ b/solution.py
@@ -42,17 +42,47 @@
     return jnp.where(target == mapped, 1.0, 0.0).astype(BF16)
 
 
+def left_half(rows):
+    return lax.broadcasted_iota(jnp.int32, (rows, LANES), 1) < HD
+
+
+def swap_halves(x):
+    return pltpu.roll(x, HD, 1)
+
+
+def merge(x, y):
+    mask = left_half(x.shape[0])
+    return jnp.where(mask, x, swap_halves(y)), jnp.where(mask, swap_halves(x), y)
+
+
+def lay_out(a_ref, b_ref, c_ref, gq_ref, gk_ref, gv_ref):
+    heads, half_main = a_ref.shape[:2]
+    rest = c_ref.shape[1] // 2
+    for i in range(heads // 2):
+        cols = slice(i * LANES, (i + 1) * LANES)
+        first, second = merge(a_ref[2 * i].astype(F32), a_ref[2 * i + 1].astype(F32))
+        gq_ref[0:half_main, cols] = first.astype(BF16)
+        gq_ref[half_main:MAIN, cols] = second.astype(BF16)
+        first, second = merge(b_ref[2 * i].astype(F32), b_ref[2 * i + 1].astype(F32))
+        gk_ref[0:MAIN, cols] = first.astype(BF16)
+        gv_ref[0:MAIN, cols] = second.astype(BF16)
+        first, second = merge(c_ref[2 * i].astype(F32), c_ref[2 * i + 1].astype(F32))
+        gk_ref[MAIN:, cols] = first[0:rest].astype(BF16)
+        gq_ref[MAIN:, cols] = first[rest:].astype(BF16)
+        gv_ref[MAIN:, cols] = second[0:rest].astype(BF16)
+
+
 def kernel(
     heads, doms,
     near_ref, send_ref, orient_ref, q_any, k_any, v_any, g_any, bias_any,
-    gq_ref, gk_ref, gv_ref,
+    a_in, b_in, c_in,
     q_ref, k_ref, v_ref, g_ref, bias_ref,
     main_out, rest_out, main_in, rest_in,
     pair_rows, qg_rows, ext, staged, arrived, turns,
     window_grads, gq_rows, total_rows, leaving, returned,
-    a_out, b_out, c_out, a_in, b_in, c_in,
+    a_out, b_out, c_out,
     inv_near, inv_send,
-    load_sem, right_sem, left_sem,
+    load_sem, keep_sem,
     in_send, in_recv, dom_send, dom_recv, back_send, back_recv, out_send, out_recv,
 ):
     grid_cols = doms // GRID_ROWS
@@ -76,15 +106,15 @@
         off = heads // 2 + half * (1 - 2 * (n % 2))
         return (me + off) % heads
 
-    right, left = (me + 1) % heads, (me + peers) % heads
-    far = heads // 2
-
     returned[:, CAP] = jnp.zeros((DIRS, BT, LANES), BF16)
 
     barrier = pltpu.get_barrier_semaphore()
-    near_count = jnp.int32(2)
-    for side in (right, left):
-        pl.semaphore_signal(barrier, inc=1, device_id={"head": side}, device_id_type=MESH)
+    near_count = jnp.int32(peers)
+
+    @pl.loop(0, peers)
+    def _(n):
+        pl.semaphore_signal(barrier, inc=1, device_id={"head": peer_of(n)}, device_id_type=MESH)
+
     for kk in range(DIRS):
         near_count = near_count + lender_ok[kk].astype(jnp.int32)
 
@@ -96,16 +126,6 @@
     loads = [pltpu.make_async_copy(src, dst, load_sem.at[n]) for n, (src, dst) in enumerate(pairs)]
     for load in loads:
         load.start()
-
-    def left_half(rows):
-        return lax.broadcasted_iota(jnp.int32, (rows, LANES), 1) < HD
-
-    def swap_halves(x):
-        return pltpu.roll(x, HD, 1)
-
-    def merge(x, y):
-        mask = left_half(x.shape[0])
-        return jnp.where(mask, x, swap_halves(y)), jnp.where(mask, swap_halves(x), y)
 
     def pack(part, first, second):
         for i in range(heads // 2):
@@ -137,30 +157,13 @@
 
     pl.semaphore_wait(barrier, near_count)
 
-    def pass_on(m):
-        pl.semaphore_signal(right_sem.at[m + 1], inc=1, device_id={"head": left}, device_id_type=MESH)
-
-        @pl.when(m + 1 < far)
-        def _():
-            pl.semaphore_signal(left_sem.at[m + 1], inc=1, device_id={"head": right}, device_id_type=MESH)
-
-    pass_on(1)
-    send_rows(0, right)
-    send_rows(0, left)
-
-    @pl.loop(2, far)
-    def _(m):
-        pl.semaphore_wait(right_sem.at[m], 1)
-        pl.semaphore_wait(left_sem.at[m], 1)
-        pass_on(m)
-        send_rows(0, (me + m) % heads)
-        send_rows(0, (me + heads - m) % heads)
+    @pl.loop(0, peers)
+    def _(n):
+        send_rows(0, peer_of(n))
 
     loads[2].wait()
     loads[3].wait()
     pack(1, q_ref, g_ref)
-    pl.semaphore_wait(right_sem.at[far], 1)
-    send_rows(0, (me + far) % heads)
 
     @pl.loop(0, peers)
     def _(n):
@@ -318,7 +321,11 @@
         peer = peer_of(n)
         home(a_out.at[peer], a_in.at[me], 0, peer).start()
 
-    a_in[me] = a_out[me]
+    keep = [
+        pltpu.make_async_copy(src.at[me], dst.at[me], keep_sem.at[n])
+        for n, (src, dst) in enumerate(((a_out, a_in), (b_out, b_in), (c_out, c_in)))
+    ]
+    keep[0].start()
 
     for b in range(QB_DOM):
         total_rows[b * BT:(b + 1) * BT] = slot_grad(b)
@@ -349,31 +356,15 @@
         home(b_out.at[peer], b_in.at[me], 1, peer).start()
         home(c_out.at[peer], c_in.at[me], 2, peer).start()
 
-    b_in[me] = b_out[me]
-    c_in[me] = c_out[me]
+    keep[1].start()
+    keep[2].start()
 
     home(a_out.at[some], a_in.at[some], 0, peer_of(0)).wait_recv()
     home(b_out.at[some], b_in.at[some], 1, peer_of(0)).wait_recv()
     home(c_out.at[some], c_in.at[some], 2, peer_of(0)).wait_recv()
 
-    @pl.loop(0, heads // 2)
-    def _(i):
-        cols = pl.ds(pl.multiple_of(i * LANES, LANES), LANES)
-        x, y = a_in[2 * i].astype(F32), a_in[2 * i + 1].astype(F32)
-        mask = left_half(half_main)
-        gq_ref[0:half_main, cols] = jnp.where(mask, x, swap_halves(y)).astype(BF16)
-        gq_ref[half_main:MAIN, cols] = jnp.where(mask, swap_halves(x), y).astype(BF16)
-        x, y = b_in[2 * i].astype(F32), b_in[2 * i + 1].astype(F32)
-        mask = left_half(MAIN)
-        gk_ref[0:MAIN, cols] = jnp.where(mask, x, swap_halves(y)).astype(BF16)
-        gv_ref[0:MAIN, cols] = jnp.where(mask, swap_halves(x), y).astype(BF16)
-        x, y = c_in[2 * i].astype(F32), c_in[2 * i + 1].astype(F32)
-        mask = left_half(4)
-        front = jnp.where(mask, x, swap_halves(y))
-        gk_ref[MAIN:count, cols] = front[0:2].astype(BF16)
-        gq_ref[MAIN:count, cols] = front[2:4].astype(BF16)
-        back = jnp.where(mask, swap_halves(x), y)
-        gv_ref[MAIN:count, cols] = back[0:2].astype(BF16)
+    for copy in keep:
+        copy.wait()
 
     for part in range(2):
         to_peer(main_out.at[part, some], main_in.at[part, some], 2 * part, peer_of(0)).wait_send()
@@ -398,15 +389,19 @@
     rest = rows - MAIN
     tokens = QB_DOM * BT
     whole = pl.BlockSpec(memory_space=pltpu.VMEM)
+    anywhere = pl.BlockSpec(memory_space=pl.ANY)
     small = pl.BlockSpec(memory_space=pltpu.SMEM)
     out = jax.ShapeDtypeStruct((rows, width), BF16)
     block = (BT, LANES)
     dma = pltpu.SemaphoreType.DMA
-    return pl.pallas_call(
+    arrivals = tuple(
+        jax.ShapeDtypeStruct((heads, n, LANES), BF16) for n in (MAIN // 2, MAIN, 2 * rest)
+    )
+    arrived = pl.pallas_call(
         functools.partial(kernel, heads, doms),
-        out_shape=(out, out, out),
-        in_specs=[small] * 3 + [pl.BlockSpec(memory_space=pl.ANY)] * 5,
-        out_specs=(whole, whole, whole),
+        out_shape=arrivals,
+        in_specs=[small] * 3 + [anywhere] * 5,
+        out_specs=(anywhere,) * 3,
         scratch_shapes=[
             *[pltpu.VMEM((rows, width), BF16)] * 4,
             pltpu.VMEM(pos_bias.shape, F32),
@@ -428,14 +423,10 @@
             pltpu.VMEM((heads, MAIN // 2, LANES), BF16),
             pltpu.VMEM((heads, MAIN, LANES), BF16),
             pltpu.VMEM((heads, 2 * rest, LANES), BF16),
-            pltpu.VMEM((heads, MAIN // 2, LANES), BF16),
-            pltpu.VMEM((heads, MAIN, LANES), BF16),
-            pltpu.VMEM((heads, 2 * rest, LANES), BF16),
             pltpu.SMEM((QB_DOM, SLOTS), jnp.int32),
             pltpu.SMEM((QB_DOM, DIRS), jnp.int32),
             dma((5,)),
-            pltpu.SemaphoreType.REGULAR((heads // 2 + 1,)),
-            pltpu.SemaphoreType.REGULAR((heads // 2 + 1,)),
+            dma((3,)),
             dma((4,)), dma((4,)),
             dma((DIRS,)), dma((DIRS,)),
             dma((DIRS,)), dma((DIRS,)),
@@ -443,6 +434,9 @@
         ],
         compiler_params=pltpu.CompilerParams(collective_id=0, has_side_effects=True),
     )(neighbours, jnp.transpose(send_block, (2, 0, 1)), orient, queries, keys_in, values_in, grad_out, pos_bias)
+    return pl.pallas_call(
+        lay_out, out_shape=(out, out, out), in_specs=[whole] * 3, out_specs=(whole, whole, whole),
+    )(*arrived)
 
 
 def solution(mesh):

time: 99.5 us -> 93.3 us (0.938)
  local copies, waits for them, and re-layouts: 3.15 us -> 0 us
  Pallas kernels: 94.6 us -> 91.5 us
    unnamed x7 -> x0, local copies, waits for them, and re-layouts: 3.15 us -> none
    pallas_call x1 -> x2, Pallas kernels: 94.6 us -> 91.5 us  [the longest x1 89.8 us: per_device(): pl.pallas_call(functools.partial(kernel, heads, doms), out_shape=arrivals...]
where the time goes in v3:
time: 93.3 us; the launch traced here: 92.2 us
  Pallas kernels  91.5 us (98%)
    pallas_call x1, Pallas kernels, per_device(): pl.pallas_call(functools.partial(kernel, heads, doms), out_shape=arrivals...  89.8 us

profile of v3, /device:TPU:1, one launch (start us, length us, event | category | flops | bytes accessed | tf_op | source)
XLA Modules:
  0.0 92.2 jit_solution(1686243542499045187)
XLA Ops:
  0.6 89.8 %shard_map.103 = (bf16[32,8,128]{2,1,0:T(8,128)(2,1)}, bf16[32,16,128]{2,1,0:T(8,128)(2,1)}, bf16[32,4,128]{2,1,0:T(4,128)(2,1)}) custom-call(s32[9,9]{1,0:T(8,128)} %near_ref.1, s32[3,1,8]{2,1,0:T(1,128)} %bitcast.1, s32[1,8]{1,0:T(1,128)} %orient_ref.1, bf16[18,2048]{1,0:T(8,128)(2,1)} %q_any.1, bf16[18,2048]{1,0:T(8,128)(2,1)} %k_any.1, ...), custom_call_target="tpu_custom_call" | custom-call | tf_op jit(solution)/shard_map/pallas_call | solution.py:400
  90.4 1.8 %shard_map.104 = (bf16[18,2048]{1,0:T(8,128)(2,1)}, bf16[18,2048]{1,0:T(8,128)(2,1)}, bf16[18,2048]{1,0:T(8,128)(2,1)}) custom-call(bf16[32,8,128]{2,1,0:T(8,128)(2,1)} %get-tuple-element.6.a_ref, bf16[32,16,128]{2,1,0:T(8,128)(2,1)} %get-tuple-element.7.b_ref, bf16[32,4,128]{2,1,0:T(4,128)(2,1)} %get-tuple-element.8.c_ref), custom_call_target="tpu_custom_call" | custom-call | tf_op jit(solution)/shard_map/pallas_call | solution.py:437

commit v4 on v3

--- a/solution.py
+++ b/solution.py
@@ -20,6 +20,8 @@
 SLOTS = QB_DOM + DIRS * CAP
 OFFSETS = [(-1, -1), (-1, 0), (-1, 1), (0, -1), (0, 1), (1, -1), (1, 0), (1, 1)]
 MESH = pl.DeviceIdType.MESH
+STAGES = [(0, 9), (9, 17), (17, 23), (23, 31)]
+STAGE_BLOCKS = [(0,), (1, 8), (2, 7), (3, 6, 4, 5)]
 F32 = jnp.float32
 BF16 = jnp.bfloat16
 
@@ -141,15 +143,15 @@
         main_in[part, me] = main_out[part, me]
         rest_in[part, me] = rest_out[part, me]
 
-    def to_peer(src, dst, sem, peer):
+    def to_peer(src, dst, sem, peer, stage=0):
         return pltpu.make_async_remote_copy(
-            src_ref=src, dst_ref=dst, send_sem=in_send.at[sem], recv_sem=in_recv.at[sem],
+            src_ref=src, dst_ref=dst, send_sem=in_send.at[sem], recv_sem=in_recv.at[sem, stage],
             device_id={"head": peer}, device_id_type=MESH,
         )
 
-    def send_rows(part, peer):
-        to_peer(main_out.at[part, peer], main_in.at[part, me], 2 * part, peer).start()
-        to_peer(rest_out.at[part, peer], rest_in.at[part, me], 2 * part + 1, peer).start()
+    def send_rows(part, peer, stage=0):
+        to_peer(main_out.at[part, peer], main_in.at[part, me], 2 * part, peer, stage).start()
+        to_peer(rest_out.at[part, peer], rest_in.at[part, me], 2 * part + 1, peer, stage).start()
 
     loads[0].wait()
     loads[1].wait()
@@ -165,9 +167,11 @@
     loads[3].wait()
     pack(1, q_ref, g_ref)
 
-    @pl.loop(0, peers)
-    def _(n):
-        send_rows(1, peer_of(n))
+    for stage, (first, last) in enumerate(STAGES):
+
+        @pl.loop(first, last)
+        def _(n):
+            send_rows(1, peer_of(n), stage)
 
     window_grads[:, WIN] = jnp.zeros((QB_DOM, BT, LANES), F32)
 
@@ -234,7 +238,22 @@
         def _():
             lend(kk).start()
 
-    unpack_rows(1, qg_rows)
+    count = MAIN + rest_in.shape[2]
+
+    def place_rows(source):
+        base = source * count
+        qg_rows[pl.ds(base, MAIN)] = main_in[1, source].astype(F32)
+        qg_rows[pl.ds(base + MAIN, count - MAIN)] = rest_in[1, source].astype(F32)
+
+    def stage_rows(stage):
+        first, last = STAGES[stage]
+        part = pl.ds(0, last - first)
+        to_peer(main_out.at[1, part], main_in.at[1, part], 2, peer_of(0), stage).wait_recv()
+        to_peer(rest_out.at[1, part], rest_in.at[1, part], 3, peer_of(0), stage).wait_recv()
+        for n in range(first, last):
+            place_rows(peer_of(n))
+
+    place_rows(me)
 
     for kk, step in enumerate(OFFSETS):
 
@@ -250,8 +269,10 @@
     lane = lax.broadcasted_iota(jnp.int32, (1, LANES), 1)
     pair_scale = jnp.where(lane < HD, scale, 1.0).astype(F32)
 
-    for b in range(QB_DOM):
-        rows = slice(b * BT, (b + 1) * BT)
+    far_block = (((me + heads // 2) % heads) * count + count // 2) // BT
+
+    def attend(b):
+        rows = pl.ds(pl.multiple_of(b * BT, BT), BT)
         qg = qg_rows[rows]
         mask = left_half(BT)
         qg2 = jnp.concatenate([jnp.where(mask, qg, 0.0), jnp.where(mask, 0.0, qg)], axis=0).astype(BF16)
@@ -272,6 +293,11 @@
         for j in range(WIN):
             window_grads[b, j] = grads[j * BT:(j + 1) * BT]
 
+    for stage, blocks in enumerate(STAGE_BLOCKS):
+        stage_rows(stage)
+        for block in blocks:
+            attend((far_block + block) % QB_DOM)
+
     def slot_grad(e):
         acc = window_grads[0, inv_near[0, e]]
         for b in range(1, QB_DOM):
@@ -308,7 +334,6 @@
             device_id={"head": peer}, device_id_type=MESH,
         )
 
-    count = MAIN + rest_in.shape[2]
     half_main = MAIN // 2
     for peer in range(heads):
         base = peer * count
@@ -427,7 +452,7 @@
             pltpu.SMEM((QB_DOM, DIRS), jnp.int32),
             dma((5,)),
             dma((3,)),
-            dma((4,)), dma((4,)),
+            dma((4,)), dma((4, len(STAGES))),
             dma((DIRS,)), dma((DIRS,)),
             dma((DIRS,)), dma((DIRS,)),
             dma((3,)), dma((3,)),

time: 93.3 us -> 92.3 us (0.989); the launches traced: 92.2 us -> 92.1 us
  no operation moved by 1% of the time
where the time goes in v4:
time: 92.3 us; the launch traced here: 92.1 us
  Pallas kernels  91.5 us (99%)
    pallas_call x1, Pallas kernels, per_device(): pl.pallas_call(functools.partial(kernel, heads, doms), out_shape=arrivals...  89.7 us

profile of v4, /device:TPU:1, one launch (start us, length us, event | category | flops | bytes accessed | tf_op | source)
XLA Modules:
  0.0 92.1 jit_solution(17564719292140702432)
XLA Ops:
  0.6 89.7 %shard_map.103 = (bf16[32,8,128]{2,1,0:T(8,128)(2,1)}, bf16[32,16,128]{2,1,0:T(8,128)(2,1)}, bf16[32,4,128]{2,1,0:T(4,128)(2,1)}) custom-call(s32[9,9]{1,0:T(8,128)} %near_ref.1, s32[3,1,8]{2,1,0:T(1,128)} %bitcast.1, s32[1,8]{1,0:T(1,128)} %orient_ref.1, bf16[18,2048]{1,0:T(8,128)(2,1)} %q_any.1, bf16[18,2048]{1,0:T(8,128)(2,1)} %k_any.1, ...), custom_call_target="tpu_custom_call" | custom-call | tf_op jit(solution)/shard_map/pallas_call | solution.py:425
  90.4 1.8 %shard_map.104 = (bf16[18,2048]{1,0:T(8,128)(2,1)}, bf16[18,2048]{1,0:T(8,128)(2,1)}, bf16[18,2048]{1,0:T(8,128)(2,1)}) custom-call(bf16[32,8,128]{2,1,0:T(8,128)(2,1)} %get-tuple-element.6.a_ref, bf16[32,16,128]{2,1,0:T(8,128)(2,1)} %get-tuple-element.7.b_ref, bf16[32,4,128]{2,1,0:T(4,128)(2,1)} %get-tuple-element.8.c_ref), custom_call_target="tpu_custom_call" | custom-call | tf_op jit(solution)/shard_map/pallas_call | solution.py:462

commit v5 on v4

--- a/solution.py
+++ b/solution.py
@@ -20,7 +20,7 @@
 SLOTS = QB_DOM + DIRS * CAP
 OFFSETS = [(-1, -1), (-1, 0), (-1, 1), (0, -1), (0, 1), (1, -1), (1, 0), (1, 1)]
 MESH = pl.DeviceIdType.MESH
-STAGES = [(0, 9), (9, 17), (17, 23), (23, 31)]
+STAGES = [(23, 31), (15, 23), (9, 15), (0, 9)]
 STAGE_BLOCKS = [(0,), (1, 8), (2, 7), (3, 6, 4, 5)]
 F32 = jnp.float32
 BF16 = jnp.bfloat16
@@ -57,9 +57,8 @@
     return jnp.where(mask, x, swap_halves(y)), jnp.where(mask, swap_halves(x), y)
 
 
-def lay_out(a_ref, b_ref, c_ref, gq_ref, gk_ref, gv_ref):
+def lay_out(a_ref, b_ref, c_ref, d_ref, gq_ref, gk_ref, gv_ref):
     heads, half_main = a_ref.shape[:2]
-    rest = c_ref.shape[1] // 2
     for i in range(heads // 2):
         cols = slice(i * LANES, (i + 1) * LANES)
         first, second = merge(a_ref[2 * i].astype(F32), a_ref[2 * i + 1].astype(F32))
@@ -69,20 +68,22 @@
         gk_ref[0:MAIN, cols] = first.astype(BF16)
         gv_ref[0:MAIN, cols] = second.astype(BF16)
         first, second = merge(c_ref[2 * i].astype(F32), c_ref[2 * i + 1].astype(F32))
-        gk_ref[MAIN:, cols] = first[0:rest].astype(BF16)
-        gq_ref[MAIN:, cols] = first[rest:].astype(BF16)
-        gv_ref[MAIN:, cols] = second[0:rest].astype(BF16)
+        gk_ref[MAIN:, cols] = first.astype(BF16)
+        gv_ref[MAIN:, cols] = second.astype(BF16)
+        first, _ = merge(d_ref[2 * i].astype(F32), d_ref[2 * i + 1].astype(F32))
+        gq_ref[MAIN:, cols] = first.astype(BF16)
 
 
 def kernel(
     heads, doms,
-    near_ref, send_ref, orient_ref, q_any, k_any, v_any, g_any, bias_any,
-    a_in, b_in, c_in,
+    near_any, send_any, orient_any, q_any, k_any, v_any, g_any, bias_any,
+    a_in, b_in, c_in, d_in,
     q_ref, k_ref, v_ref, g_ref, bias_ref,
     main_out, rest_out, main_in, rest_in,
     pair_rows, qg_rows, ext, staged, arrived, turns,
     window_grads, gq_rows, total_rows, leaving, returned,
-    a_out, b_out, c_out,
+    a_out, b_out, c_out, d_out,
+    near_ref, send_ref, orient_ref,
     inv_near, inv_send,
     load_sem, keep_sem,
     in_send, in_recv, dom_send, dom_recv, back_send, back_recv, out_send, out_recv,
@@ -124,7 +125,8 @@
         def _():
             pl.semaphore_signal(barrier, inc=1, device_id={"dom": lender[kk]}, device_id_type=MESH)
 
-    pairs = ((k_any, k_ref), (v_any, v_ref), (q_any, q_ref), (g_any, g_ref), (bias_any, bias_ref))
+    pairs = ((k_any, k_ref), (v_any, v_ref), (q_any, q_ref), (g_any, g_ref), (bias_any, bias_ref),
+             (near_any, near_ref), (send_any, send_ref), (orient_any, orient_ref))
     loads = [pltpu.make_async_copy(src, dst, load_sem.at[n]) for n, (src, dst) in enumerate(pairs)]
     for load in loads:
         load.start()
@@ -167,13 +169,16 @@
     loads[3].wait()
     pack(1, q_ref, g_ref)
 
-    for stage, (first, last) in enumerate(STAGES):
+    for stage, (first, last) in reversed(list(enumerate(STAGES))):
 
         @pl.loop(first, last)
         def _(n):
             send_rows(1, peer_of(n), stage)
 
     window_grads[:, WIN] = jnp.zeros((QB_DOM, BT, LANES), F32)
+
+    for load in loads[5:]:
+        load.wait()
 
     def lent_block(kk, c):
         if live_slots(*OFFSETS[kk]) == CAP:
@@ -269,7 +274,7 @@
     lane = lax.broadcasted_iota(jnp.int32, (1, LANES), 1)
     pair_scale = jnp.where(lane < HD, scale, 1.0).astype(F32)
 
-    far_block = (((me + heads // 2) % heads) * count + count // 2) // BT
+    far_block = (me * count + count // 2) // BT
 
     def attend(b):
         rows = pl.ds(pl.multiple_of(b * BT, BT), BT)
@@ -340,17 +345,20 @@
         first = gq_rows[base:base + half_main]
         second = gq_rows[base + half_main:base + MAIN]
         a_out[peer] = jnp.where(left_half(half_main), first, swap_halves(second)).astype(BF16)
+        d_out[peer] = gq_rows[base + MAIN:base + count].astype(BF16)
 
     @pl.loop(0, peers)
     def _(n):
         peer = peer_of(n)
         home(a_out.at[peer], a_in.at[me], 0, peer).start()
+        home(d_out.at[peer], d_in.at[me], 3, peer).start()
 
     keep = [
         pltpu.make_async_copy(src.at[me], dst.at[me], keep_sem.at[n])
-        for n, (src, dst) in enumerate(((a_out, a_in), (b_out, b_in), (c_out, c_in)))
+        for n, (src, dst) in enumerate(((a_out, a_in), (b_out, b_in), (c_out, c_in), (d_out, d_in)))
     ]
     keep[0].start()
+    keep[3].start()
 
     for b in range(QB_DOM):
         total_rows[b * BT:(b + 1) * BT] = slot_grad(b)
@@ -370,10 +378,7 @@
     for peer in range(heads):
         base = peer * count
         b_out[peer] = total_rows[base:base + MAIN].astype(BF16)
-        rest = total_rows[base + MAIN:base + count]
-        c_out[peer, 0:2] = rest.astype(BF16)
-        rest = gq_rows[base + MAIN:base + count]
-        c_out[peer, 2:4] = rest.astype(BF16)
+        c_out[peer] = total_rows[base + MAIN:base + count].astype(BF16)
 
     @pl.loop(0, peers)
     def _(n):
@@ -387,6 +392,7 @@
     home(a_out.at[some], a_in.at[some], 0, peer_of(0)).wait_recv()
     home(b_out.at[some], b_in.at[some], 1, peer_of(0)).wait_recv()
     home(c_out.at[some], c_in.at[some], 2, peer_of(0)).wait_recv()
+    home(d_out.at[some], d_in.at[some], 3, peer_of(0)).wait_recv()
 
     for copy in keep:
         copy.wait()
@@ -407,6 +413,7 @@
     home(a_out.at[some], a_in.at[some], 0, peer_of(0)).wait_send()
     home(b_out.at[some], b_in.at[some], 1, peer_of(0)).wait_send()
     home(c_out.at[some], c_in.at[some], 2, peer_of(0)).wait_send()
+    home(d_out.at[some], d_in.at[some], 3, peer_of(0)).wait_send()
 
 
 def per_device(heads, doms, queries, keys_in, values_in, grad_out, pos_bias, neighbours, send_block, orient):
@@ -415,18 +422,17 @@
     tokens = QB_DOM * BT
     whole = pl.BlockSpec(memory_space=pltpu.VMEM)
     anywhere = pl.BlockSpec(memory_space=pl.ANY)
-    small = pl.BlockSpec(memory_space=pltpu.SMEM)
     out = jax.ShapeDtypeStruct((rows, width), BF16)
     block = (BT, LANES)
     dma = pltpu.SemaphoreType.DMA
     arrivals = tuple(
-        jax.ShapeDtypeStruct((heads, n, LANES), BF16) for n in (MAIN // 2, MAIN, 2 * rest)
+        jax.ShapeDtypeStruct((heads, n, LANES), BF16) for n in (MAIN // 2, MAIN, rest, rest)
     )
     arrived = pl.pallas_call(
         functools.partial(kernel, heads, doms),
         out_shape=arrivals,
-        in_specs=[small] * 3 + [anywhere] * 5,
-        out_specs=(anywhere,) * 3,
+        in_specs=[anywhere] * 8,
+        out_specs=(anywhere,) * 4,
         scratch_shapes=[
             *[pltpu.VMEM((rows, width), BF16)] * 4,
             pltpu.VMEM(pos_bias.shape, F32),
@@ -447,20 +453,24 @@
             pltpu.VMEM((DIRS, CAP + 1) + block, BF16),
             pltpu.VMEM((heads, MAIN // 2, LANES), BF16),
             pltpu.VMEM((heads, MAIN, LANES), BF16),
-            pltpu.VMEM((heads, 2 * rest, LANES), BF16),
+            pltpu.VMEM((heads, rest, LANES), BF16),
+            pltpu.VMEM((heads, rest, LANES), BF16),
+            pltpu.SMEM((QB_DOM, WIN), jnp.int32),
+            pltpu.SMEM((CAP, 1, DIRS), jnp.int32),
+            pltpu.SMEM((1, DIRS), jnp.int32),
             pltpu.SMEM((QB_DOM, SLOTS), jnp.int32),
             pltpu.SMEM((QB_DOM, DIRS), jnp.int32),
-            dma((5,)),
-            dma((3,)),
+            dma((8,)),
+            dma((4,)),
             dma((4,)), dma((4, len(STAGES))),
             dma((DIRS,)), dma((DIRS,)),
             dma((DIRS,)), dma((DIRS,)),
-            dma((3,)), dma((3,)),
+            dma((4,)), dma((4,)),
         ],
         compiler_params=pltpu.CompilerParams(collective_id=0, has_side_effects=True),
     )(neighbours, jnp.transpose(send_block, (2, 0, 1)), orient, queries, keys_in, values_in, grad_out, pos_bias)
     return pl.pallas_call(
-        lay_out, out_shape=(out, out, out), in_specs=[whole] * 3, out_specs=(whole, whole, whole),
+        lay_out, out_shape=(out, out, out), in_specs=[whole] * 4, out_specs=(whole, whole, whole),
     )(*arrived)
 
 

time: 92.3 us -> 90.2 us (0.977)
  Pallas kernels: 91.5 us -> 88.7 us
    pallas_call x1, Pallas kernels: 89.7 us -> 87 us  [per_device(): pl.pallas_call(functools.partial(kernel, heads, doms), out_shape=arrivals...]
where the time goes in v5:
time: 90.2 us; the launch traced here: 89.4 us
  Pallas kernels  88.7 us (98%)
    pallas_call x1, Pallas kernels, per_device(): pl.pallas_call(functools.partial(kernel, heads, doms), out_shape=arrivals...  87 us

profile of v5, /device:TPU:1, one launch (start us, length us, event | category | flops | bytes accessed | tf_op | source)
XLA Modules:
  0.0 89.4 jit_solution(2149625654293326185)
XLA Ops:
  0.6 87.0 %shard_map.103 = (bf16[32,8,128]{2,1,0:T(8,128)(2,1)}, bf16[32,16,128]{2,1,0:T(8,128)(2,1)}, bf16[32,2,128]{2,1,0:T(2,128)(2,1)}, bf16[32,2,128]{2,1,0:T(2,128)(2,1)}) custom-call(s32[9,9]{1,0:T(8,128)} %near_any.1, s32[3,1,8]{2,1,0:T(1,128)} %bitcast.1, s32[1,8]{1,0:T(1,128)} %orient_any.1, bf16[18,2048]{1,0:T(8,128)(2,1)} %q_any.1, ...), custom_call_target="tpu_custom_call" | custom-call | tf_op jit(solution)/shard_map/pallas_call | solution.py:431
  87.6 1.8 %shard_map.104 = (bf16[18,2048]{1,0:T(8,128)(2,1)}, bf16[18,2048]{1,0:T(8,128)(2,1)}, bf16[18,2048]{1,0:T(8,128)(2,1)}) custom-call(bf16[32,8,128]{2,1,0:T(8,128)(2,1)} %get-tuple-element.7.a_ref, bf16[32,16,128]{2,1,0:T(8,128)(2,1)} %get-tuple-element.8.b_ref, bf16[32,2,128]{2,1,0:T(2,128)(2,1)} %get-tuple-element.9.c_ref, ...), custom_call_target="tpu_custom_call" | custom-call | tf_op jit(solution)/shard_map/pallas_call | solution.py:472

commit v6 on v5

--- a/solution.py
+++ b/solution.py
@@ -20,8 +20,8 @@
 SLOTS = QB_DOM + DIRS * CAP
 OFFSETS = [(-1, -1), (-1, 0), (-1, 1), (0, -1), (0, 1), (1, -1), (1, 0), (1, 1)]
 MESH = pl.DeviceIdType.MESH
-STAGES = [(23, 31), (15, 23), (9, 15), (0, 9)]
-STAGE_BLOCKS = [(0,), (1, 8), (2, 7), (3, 6, 4, 5)]
+STAGES = [(23, 31), (15, 23), (9, 15), (3, 9), (0, 3)]
+STAGE_BLOCKS = [(0,), (1, 8), (2, 7), (3, 6), (4, 5)]
 F32 = jnp.float32
 BF16 = jnp.bfloat16
 

time: 90.2 us -> 90.4 us (level)
  no operation moved by 1% of the time
where the time goes in v6:
time: 90.4 us; the launch traced here: 89.6 us
  Pallas kernels  88.9 us (98%)
    pallas_call x1, Pallas kernels, per_device(): pl.pallas_call(functools.partial(kernel, heads, doms), out_shape=arrivals...  87.2 us

profile of v6, /device:TPU:1, one launch (start us, length us, event | category | flops | bytes accessed | tf_op | source)
XLA Modules:
  0.0 89.6 jit_solution(14180704756761688261)
XLA Ops:
  0.6 87.2 %shard_map.103 = (bf16[32,8,128]{2,1,0:T(8,128)(2,1)}, bf16[32,16,128]{2,1,0:T(8,128)(2,1)}, bf16[32,2,128]{2,1,0:T(2,128)(2,1)}, bf16[32,2,128]{2,1,0:T(2,128)(2,1)}) custom-call(s32[9,9]{1,0:T(8,128)} %near_any.1, s32[3,1,8]{2,1,0:T(1,128)} %bitcast.1, s32[1,8]{1,0:T(1,128)} %orient_any.1, bf16[18,2048]{1,0:T(8,128)(2,1)} %q_any.1, ...), custom_call_target="tpu_custom_call" | custom-call | tf_op jit(solution)/shard_map/pallas_call | solution.py:431
  87.8 1.8 %shard_map.104 = (bf16[18,2048]{1,0:T(8,128)(2,1)}, bf16[18,2048]{1,0:T(8,128)(2,1)}, bf16[18,2048]{1,0:T(8,128)(2,1)}) custom-call(bf16[32,8,128]{2,1,0:T(8,128)(2,1)} %get-tuple-element.7.a_ref, bf16[32,16,128]{2,1,0:T(8,128)(2,1)} %get-tuple-element.8.b_ref, bf16[32,2,128]{2,1,0:T(2,128)(2,1)} %get-tuple-element.9.c_ref, ...), custom_call_target="tpu_custom_call" | custom-call | tf_op jit(solution)/shard_map/pallas_call | solution.py:472
